TPU v7x, 256 devices: a whole 4x4x8 slice. The times are simulated.
256 devices in a mesh: wide: 32 (over x, y, core), narrow: 8 (over z).
Axes of the slice: x: 4, y: 4, z: 8, core: 2. Of those that a mesh axis runs over, the one named last changes fastest.
Arguments:
- sources: float32 [32, 8, 16, 2, 512], P('wide', 'narrow'), may hold values from -6 to 6
- schur_blocks: bfloat16 [32, 8, 2048, 2048], P('wide', 'narrow'), as said below
- scaling: float32 [32, 8, 2, 512], P('wide', 'narrow'), may hold values from 0.08 to 0.4
- coarse_basis: float32 [32, 8, 2, 2, 8, 512], P('wide', 'narrow'), may hold values from -0.09375 to 0.09375
- coarse_inverse: float32 [32, 80, 80], P('wide'), as said below
- face_sizes: int32 [32, 8, 2], P('wide', 'narrow'), may hold values from 0 to 512, as said below
- face_match: int32 [32, 8, 2, 512], P('wide', 'narrow'), may hold values from 0 to 511, as said below
- face_slots: int32 [32, 8, 4], P('wide', 'narrow'), may hold values from 0 to 3, each once within a row
- corner_slots: int32 [33, 9], replicated, may hold values from 0 to 319, as said below
Outputs:
- solution: float32 [32, 8, 16, 2, 512], P('wide', 'narrow')
- residual: float32 [32, 8, 16, 2, 512], P('wide', 'narrow')
Inputs may be any that keep to these rules, and one draw needn't show every extreme that they name: `face_sizes`: the east faces of the last wide index and the north faces of the last narrow index have 0 unknowns; every other face has 128 to 512, and some face has exactly 512. `face_match`: each block is a permutation of 0 to 511 that maps the positions below the size of the matching owned face onto themselves. `corner_slots`: distinct slots for distinct vertices; slot 319 is used. `schur_blocks`: each block is symmetric and positive definite. `coarse_inverse`: each block is symmetric and positive definite.
All inputs are finite; a program needn't handle non-finite values.
Results may differ from a plain program's by a relative error of at most 0.0052.
Values may be sent and summed in bfloat16 or wider, within the bound.
A program may use at most 64 MiB of HBM per device.

v0:
```python
import jax
import jax.numpy as jnp
from jax import lax
from jax.sharding import PartitionSpec as P

ITERS = 2


highest = lax.Precision.HIGHEST


def shifted(block, axis, distance):
    devices = range(lax.axis_size(axis))
    route = [(i - distance, i) for i in devices if i - distance in devices]
    return lax.ppermute(block, axis, route)


def body(
    sources,
    schur_blocks,
    scaling,
    coarse_basis,
    coarse_inverse,
    face_sizes,
    face_match,
    face_slots,
    corner_slots,
):
    wide_count = lax.axis_size("wide")
    wide_at = lax.axis_index("wide")
    narrow_at = lax.axis_index("narrow")
    nrhs_count = sources.shape[2]
    face_width = sources.shape[4]
    basis_count = coarse_basis.shape[4]
    block_order = coarse_inverse.shape[1]
    capacity = block_order // basis_count
    slot_count = capacity * wide_count
    places = lax.broadcasted_iota(jnp.int32, (2, face_width), 1)
    live_mask = (places < face_sizes[0, 0][:, None]).astype(jnp.float32)
    weights = scaling[0, 0] * live_mask
    vectors = coarse_basis[0, 0] * live_mask[:, None, None, :]
    forward = face_match[0, 0]
    source_rows = lax.broadcasted_iota(jnp.int32, (2, face_width, face_width), 1)
    match_table = (forward[:, None, :] == source_rows).astype(jnp.float32)
    match_narrow = match_table.astype(jnp.bfloat16)
    slot_table = (face_slots[0, 0][:, None] == jnp.arange(4, dtype=jnp.int32)[None, :]).astype(
        jnp.float32
    )
    matrix = schur_blocks[0, 0]
    square = lax.dynamic_slice(corner_slots, (wide_at, narrow_at), (2, 2))
    corner_ids = jnp.stack([square[1, 0], square[1, 1], square[0, 1], square[1, 1]])
    incidence = (corner_ids[:, None] == jnp.arange(slot_count, dtype=jnp.int32)[None, :]).astype(
        jnp.float32
    )
    inverse_block = coarse_inverse[0]
    initial = sources[0, 0] * live_mask[None]

    def finish(residual, solved_slots):
        local_values = jnp.dot(
            incidence, solved_slots, precision=highest, preferred_element_type=jnp.float32
        )
        local_values = local_values.reshape(2, 2, basis_count, nrhs_count)
        return weights[None] * residual + jnp.einsum(
            "femk,femr->rfk", vectors, local_values, precision=highest
        )

    def precondition(residual):
        partial_value = jnp.einsum("femk,rfk->femr", vectors, residual, precision=highest).reshape(
            4, basis_count * nrhs_count
        )
        dense_part = jnp.dot(
            incidence.T, partial_value, precision=highest, preferred_element_type=jnp.float32
        )
        owned_rows = lax.psum_scatter(dense_part, "wide", scatter_dimension=0, tiled=True)
        owner_block = lax.psum(owned_rows, "narrow").reshape(block_order, nrhs_count)
        solved = jnp.dot(
            inverse_block, owner_block, precision=highest, preferred_element_type=jnp.float32
        )
        all_solved = lax.all_gather(
            solved.reshape(capacity, basis_count * nrhs_count), "wide", axis=0, tiled=True
        )
        precond = finish(residual, all_solved)
        inner_value = lax.psum(jnp.sum(residual * precond, axis=(1, 2)), ("wide", "narrow"))
        return (precond, inner_value)

    residual = initial
    solution = jnp.zeros_like(initial)
    precond, inner_now = precondition(residual)
    direction = precond
    for iteration in range(ITERS):
        rounded = direction.astype(jnp.bfloat16)
        from_west = shifted(rounded[:, 0], "wide", 1)
        from_south = shifted(rounded[:, 1], "narrow", 1)
        west_face = jnp.dot(from_west, match_narrow[0], preferred_element_type=jnp.float32)
        south_face = jnp.dot(from_south, match_narrow[1], preferred_element_type=jnp.float32)
        stacked = jnp.stack(
            [
                rounded[:, 0].astype(jnp.float32),
                rounded[:, 1].astype(jnp.float32),
                west_face,
                south_face,
            ],
            axis=1,
        )
        slotted = jnp.einsum("rdk,ds->rsk", stacked, slot_table, precision=highest).astype(
            jnp.bfloat16
        )
        product = jnp.dot(
            slotted.reshape(nrhs_count, 4 * face_width), matrix, preferred_element_type=jnp.float32
        )
        by_face = jnp.einsum(
            "rsk,ds->rdk", product.reshape(nrhs_count, 4, face_width), slot_table, precision=highest
        )
        to_west = jnp.einsum("rk,mk->rm", by_face[:, 2], match_table[0], precision=highest)
        to_south = jnp.einsum("rk,mk->rm", by_face[:, 3], match_table[1], precision=highest)
        from_east = shifted(to_west, "wide", -1)
        from_north = shifted(to_south, "narrow", -1)
        summed_all = jnp.stack([by_face[:, 0] + from_east, by_face[:, 1] + from_north], axis=1)
        applied = summed_all * live_mask[None]
        curvature = lax.psum(jnp.sum(direction * applied, axis=(1, 2)), ("wide", "narrow"))
        step_size = inner_now / curvature
        solution = solution + step_size[:, None, None] * direction
        residual = residual - step_size[:, None, None] * applied
        if iteration + 1 < ITERS:
            precond, inner_new = precondition(residual)
            direction = precond + (inner_new / inner_now)[:, None, None] * direction
            inner_now = inner_new
    return (solution[None, None], residual[None, None])


def solution(mesh):
    placed = (
        P("wide", "narrow", None, None, None),
        P("wide", "narrow", None, None),
        P("wide", "narrow", None, None),
        P("wide", "narrow", None, None, None, None),
        P("wide", None, None),
        P("wide", "narrow", None),
        P("wide", "narrow", None, None),
        P("wide", "narrow", None),
        P(),
    )
    return jax.shard_map(
        body,
        mesh=mesh,
        in_specs=placed,
        out_specs=(P("wide", "narrow", None, None, None), P("wide", "narrow", None, None, None)),
        check_vma=False,
    )
```

profile of v0, /device:TPU:1, one launch (start us, length us, event | category | flops | bytes accessed | tf_op | source)
XLA Modules:
  0.0 640.1 jit_solution(5082868968421109135)
XLA Ops:
  7.2 0.8 dynamic_slice.3
  9.4 1.1 fusion.22
  10.6 2.1 pad_add_fusion
  12.6 1.1 fusion.46
  14.5 1.3 dynamic-slice
  16.4 110.0 %all-reduce.6.cloned.1.call-done = f32[320,128]{1,0:T(8,128)} async-done(((f32[320,128]{1,0:T(8,128)}), f32[320,128]{1,0:T(8,128)}) %all-reduce.6.cloned.1.call-update) | async-done | bytes 163856
  127.2 23.5 %psum.42 = f32[80,16]{1,0:T(8,128)S(1)} all-reduce(f32[80,16]{1,0:T(8,128)S(1)} %reshape.170), channel_id=1, replica_groups=mesh['wide'=32,'narrow'=8] {'narrow'}, use_global_device_ids=true, to_apply=%region_1.0 | all-reduce | flops 1280 | bytes 10240 | tf_op jit(solution)/shard_map/psum | solution.py:75
  151.1 30.1 %all-gather = f32[32,10,128]{2,1,0:T(8,128)S(1)} all-gather(f32[1,10,128]{2,1,0:T(8,128)S(1)} %reshape.179), channel_id=1, replica_groups=mesh['wide'=32,'narrow'=8] {'wide'}, dimensions={0}, use_global_device_ids=true | all-gather | bytes 168960 | tf_op jit(solution)/shard_map/all_gather | solution.py:79
  181.6 1.1 fusion.59
  182.7 1.3 collective-permute-start.1
  184.1 1.2 convert_convert_fusion
  185.3 12.3 %copy.57 = bf16[2048,2048]{1,0:T(8,128)(2,1)} copy(bf16[2048,2048]{0,1:T(8,128)(2,1)} %bitcast.206) | data formatting | bytes 16777216 | tf_op jit(solution)/shard_map/dot_general | solution.py:108
  197.6 2.6 collective-permute-start
  201.7 5.6 fusion.60
  208.9 1.3 collective-permute-start.3
  210.2 1.9 collective-permute-start.2
  212.1 2.1 collective-permute-done.3
  214.2 1.7 collective-permute-done.2
  216.1 78.5 %all-reduce.2 = (f32[16]{0:T(128)S(1)}, f32[16]{0:T(128)S(1)}) all-reduce(f32[16]{0:T(128)S(1)} %get-tuple-element.9, f32[16]{0:T(128)S(1)} %get-tuple-element.8), channel_id=1, replica_groups=mesh['wide'=32,'narrow'=8] {'wide','narrow'}, use_global_device_ids=true, to_apply=%region_3.0 | all-reduce | flops 32 | bytes 256 | tf_op jit(solution)/shard_map/psum | solution.py:83
  295.0 1.1 fusion.44
  296.1 106.8 %all-reduce.8.cloned.1.call-done = f32[320,128]{1,0:T(8,128)} async-done(((f32[320,128]{1,0:T(8,128)}), f32[320,128]{1,0:T(8,128)}) %all-reduce.8.cloned.1.call-update) | async-done | bytes 163856
  403.7 23.5 %psum.45 = f32[80,16]{1,0:T(8,128)S(1)} all-reduce(f32[80,16]{1,0:T(8,128)S(1)} %reshape.175), channel_id=1, replica_groups=mesh['wide'=32,'narrow'=8] {'narrow'}, use_global_device_ids=true, to_apply=%region_7.0 | all-reduce | flops 1280 | bytes 10240 | tf_op jit(solution)/shard_map/psum | solution.py:75
  427.6 30.1 %all-gather.1 = f32[32,10,128]{2,1,0:T(8,128)S(1)} all-gather(f32[1,10,128]{2,1,0:T(8,128)S(1)} %reshape.181), channel_id=1, replica_groups=mesh['wide'=32,'narrow'=8] {'wide'}, dimensions={0}, use_global_device_ids=true | all-gather | bytes 168960 | tf_op jit(solution)/shard_map/all_gather | solution.py:79
  458.5 73.3 %psum.46 = f32[16]{0:T(128)S(1)} all-reduce(f32[16]{0:T(128)S(1)} %get-tuple-element.39), channel_id=1, replica_groups=mesh['wide'=32,'narrow'=8] {'wide','narrow'}, use_global_device_ids=true, to_apply=%region_9.0 | all-reduce | flops 16 | bytes 128 | tf_op jit(solution)/shard_map/psum | solution.py:83
  531.9 2.4 collective-permute-start.4
  534.4 3.9 collective-permute-start.5
  539.5 5.6 fusion.61
  546.7 1.3 collective-permute-start.7
  548.0 2.7 collective-permute-start.6
  550.8 0.9 collective-permute-done.7
  551.6 1.6 collective-permute-done.6
  553.5 78.3 %psum.47 = f32[16]{0:T(128)S(1)} all-reduce(f32[16]{0:T(128)S(1)} %fusion.15), channel_id=1, replica_groups=mesh['wide'=32,'narrow'=8] {'wide','narrow'}, use_global_device_ids=true, to_apply=%region_11.0 | all-reduce | flops 16 | bytes 128 | tf_op jit(solution)/shard_map/psum | solution.py:120
  (71 shorter events, 13.8 us)
Async XLA Ops:
  7.2 143.6 %copy-start = (f32[1,80,80]{2,1,0:T(8,128)S(1)}, f32[1,80,80]{2,1,0:T(8,128)}, u32[]{:S(2)}) copy-start(f32[1,80,80]{2,1,0:T(8,128)} %param.13) | copy-start | bytes 76804
  7.2 119.2 %all-reduce.6.cloned.1.call-start = ((), (), s32[]{:S(2)}) async-start(), calls=%async_computation | async-start | bytes 327680
  13.7 389.2 %all-reduce.8.cloned.1.call-start = ((), (), s32[]{:S(2)}) async-start(), calls=%async_computation.1 | async-start | bytes 327680
  182.7 17.5 %collective-permute-start.1 = (bf16[16,512]{1,0:T(8,128)(2,1)S(1)}, bf16[16,512]{1,0:T(8,128)(2,1)S(1)}, u32[]{:S(2)}, u32[]{:S(2)}) collective-permute-start(bf16[16,512]{1,0:T(8,128)(2,1)S(1)} %get-tuple-element.30), channel_id=1, source_target_pairs={{0,1},{1,2},{2,3},{3,4},{4,5},{5,6},{6,7},{8,9},{9,10},{10,11},{11... | collective-permute-start | bytes 49160 | tf_op jit(solution)/shard_map/ppermute | solution.py:15
  185.3 16.0 %copy-start.3 = (s32[1,1,4]{2,1,0:T(1,128)S(1)}, s32[1,1,4]{2,1,0:T(1,128)}, u32[]{:S(2)}) copy-start(s32[1,1,4]{2,1,0:T(1,128)} %param.16) | copy-start | bytes 52
  197.6 18.4 %copy-start.1 = (f32[1,1,16,2,512]{4,3,2,1,0:T(2,128)S(1)}, f32[1,1,16,2,512]{4,3,2,1,0:T(2,128)}, u32[]{:S(2)}) copy-start(f32[1,1,16,2,512]{4,3,2,1,0:T(2,128)} %param.9) | copy-start | bytes 196612
  197.6 97.1 %copy-start.2 = (f32[1,1,2,2,8,512]{5,4,3,2,1,0:T(8,128)S(1)}, f32[1,1,2,2,8,512]{5,4,3,2,1,0:T(8,128)}, u32[]{:S(2)}) copy-start(f32[1,1,2,2,8,512]{5,4,3,2,1,0:T(8,128)} %param.12) | copy-start | bytes 196612
  197.6 3.4 collective-permute-start
  208.9 5.4 collective-permute-start.3
  210.2 5.8 collective-permute-start.2
  531.9 6.3 collective-permute-start.4
  534.4 4.5 collective-permute-start.5
  546.7 4.9 collective-permute-start.7
  548.0 5.2 collective-permute-start.6
Sparse Core Ops, SparseCore 0:
  13.8 112.5 all-reduce.5
  296.3 106.6 all-reduce.7
where the time goes:
time: 641 us; the launch traced here: 640 us
  blocking collectives  337 us (53%)
  waiting for transfers between devices  224 us (35%)
  matrix products  21.5 us (3%)
  local copies, waits for them, and re-layouts  18.9 us (3%)
  starting transfers between devices  17.5 us (3%)
  between operations  15 us (2%)
    unnamed x4, waiting for transfers between devices  217 us
    psum x2, blocking collectives, precondition(): lax.psum(jnp.sum(residual * precond, axis=(1, 2)), ('wide', 'narrow'))  152 us
    psum x1, blocking collectives, body(): lax.psum(jnp.sum(direction * applied, axis=(1, 2)), ('wide', 'narrow'))  78.3 us
    all_gather x2, blocking collectives, precondition(): lax.all_gather(solved.reshape(capacity, basis_count * nrhs_count), 'wide'...  60.2 us
    psum x2, blocking collectives, precondition(): lax.psum(owned_rows, 'narrow').reshape(block_order, nrhs_count)  47.1 us
    ppermute x8, starting transfers between devices, shifted(): return lax.ppermute(block, axis, route)  17.5 us
  transfers between devices with their start and end apart: 10, of which 8 were waited for; matrix products, arithmetic and copies ran while one was open for 2% of the time, Pallas kernels for 0%

commit v1 on v0

v1 whole, which is shorter than its diff:
```python
import jax
import jax.numpy as jnp
from jax import lax
from jax.experimental import pallas as pl
from jax.experimental.pallas import tpu as pltpu
from jax.sharding import PartitionSpec as P

MESH = pl.DeviceIdType.MESH
f32 = jnp.float32
bf16 = jnp.bfloat16
NT = (((1,), (1,)), ((), ()))
EAST, NORTH, WEST, SOUTH = range(4)


def iota(shape, dim):
    return lax.broadcasted_iota(jnp.int32, shape, dim)


def mm(a, b):
    return jnp.dot(a, b, preferred_element_type=f32)


def mm_nt(a, b):
    return lax.dot_general(a, b, NT, preferred_element_type=f32)


def split(x):
    high = x.astype(bf16)
    return high, (x - high.astype(f32)).astype(bf16)


def halves(x):
    return jnp.concatenate(split(x), axis=0)


def fold(x):
    rows = x.shape[0] // 2
    return x[:rows] + x[rows:]


def kernel(
    sizes,
    slots,
    corners,
    src,
    schur,
    scaling,
    basis,
    inverse,
    match,
    row_slots,
    sol_out,
    res_out,
    blocks,
    faces,
    lift,
    perm,
    pick,
    coef,
    inverses,
    zmsg,
    zbuf,
    wmsg,
    wbuf,
    zlast,
    zlast_buf,
    wlast,
    wlast_buf,
    fore_out,
    fore_in,
    flux_out,
    flux_in,
    back_out,
    back_in,
    load_sem,
    z_send,
    z_recv,
    w_send,
    w_recv,
    fore_send,
    fore_recv,
    flux_send,
    flux_recv,
    back_send,
    back_recv,
    inv_send,
    inv_recv,
):
    wide_count = lax.axis_size("wide")
    narrow_count = lax.axis_size("narrow")
    wide_at = lax.axis_index("wide")
    narrow_at = lax.axis_index("narrow")
    count = src.shape[0]
    width = src.shape[2]
    order = inverse.shape[0]
    modes = basis.shape[2]
    capacity = order // modes
    lanes = modes * count
    corner_rows = 4 * modes
    msg_rows = wmsg.shape[1]

    def z_peer(k):
        return (wide_at, lax.rem(narrow_at + 1 + k, narrow_count))

    def w_peer(k):
        return (lax.rem(wide_at + 1 + k, wide_count), narrow_at)

    east = (lax.rem(wide_at + 1, wide_count), narrow_at)
    west = (lax.rem(wide_at + wide_count - 1, wide_count), narrow_at)
    north = (wide_at, lax.rem(narrow_at + 1, narrow_count))
    south = (wide_at, lax.rem(narrow_at + narrow_count - 1, narrow_count))

    barrier = pltpu.get_barrier_semaphore()

    def greet(peer, number):
        def one(k, carry):
            pl.semaphore_signal(barrier, 1, device_id=peer(k), device_id_type=MESH)
            return carry

        lax.fori_loop(0, number, one, 0)

    greet(z_peer, narrow_count - 1)
    greet(w_peer, wide_count - 1)

    for s in range(4):
        for t in range(4):
            pltpu.make_async_copy(
                schur.at[pl.ds(s * width, width), pl.ds(t * width, width)],
                blocks.at[s, t],
                load_sem,
            ).start()

    def remote(a, b, send, recv, device):
        return pltpu.make_async_remote_copy(
            src_ref=a, dst_ref=b, send_sem=send, recv_sem=recv, device_id=device, device_id_type=MESH
        )

    def spread(a, b, send, recv, peer, number):
        def one(k, carry):
            remote(a, b, send, recv, peer(k)).start()
            return carry

        lax.fori_loop(0, number, one, 0)

    def drain(ref, number, sem):
        part = ref.at[pl.ds(0, number)]
        pltpu.make_async_copy(part, part, sem).wait()

    place = iota((1, width), 1)
    live = [(place < sizes[0, f]).astype(f32) for f in range(2)]
    weight = [scaling[f : f + 1, :] * live[f] for f in range(2)]
    residual = [src[:, f, :] * live[f] for f in range(2)]
    scaled = [residual[f] * weight[f] for f in range(2)]
    vec = [[basis[f, e] * live[f] for e in range(2)] for f in range(2)]
    nothing = jnp.zeros((modes, width), f32)

    for f in range(2):
        fore_out[f, 0 : 2 * count, :] = halves(scaled[f])
        fore_out[f, 2 * count : 4 * count, :] = halves(jnp.concatenate(vec[f], axis=0))

    def set_face(d, scaled_parts, ends):
        faces[d, 0 : 2 * count, :] = scaled_parts
        faces[d, 2 * count : 2 * count + 2 * corner_rows, :] = ends

    set_face(
        EAST,
        halves(scaled[0]),
        halves(jnp.concatenate([nothing, nothing, vec[0][0], vec[0][1]], axis=0)),
    )
    set_face(
        NORTH,
        halves(scaled[1]),
        halves(jnp.concatenate([nothing, vec[1][0], nothing, vec[1][1]], axis=0)),
    )

    wide_lanes = 4 * lanes
    grow = ((iota((2 * corner_rows, wide_lanes), 0) & (corner_rows - 1)) == iota((2 * corner_rows, wide_lanes), 1) // count).astype(bf16)
    own_lane = iota((count, wide_lanes), 1) % count == iota((count, wide_lanes), 0)
    own_lane_one = own_lane[:, 0:lanes]

    def restrict(pairs):
        total = 0.0
        for values, d in pairs:
            total = total + mm_nt(
                halves(values), faces[d, 2 * count : 2 * count + 2 * corner_rows, :]
            )
        spread_out = fold(mm(halves(fold(total)), grow))
        row = jnp.sum(jnp.where(own_lane, spread_out, 0.0), axis=0, keepdims=True)
        return jnp.concatenate([row[:, v * lanes : (v + 1) * lanes] for v in range(4)], axis=0)

    def inner(pairs):
        total = 0.0
        for a, b in pairs:
            total = total + jnp.sum(a * b, axis=1, keepdims=True)
        return total

    lane_one = iota((count, lanes), 1)
    row_one = iota((count, lanes), 0)

    def pack(values):
        out = jnp.zeros((count, lanes), f32)
        for g, value in enumerate(values):
            out = out + jnp.where(lane_one == g * count + row_one, value, 0.0)
        return jnp.sum(out, axis=0, keepdims=True)

    def unpack(row, g):
        return jnp.sum(jnp.where(lane_one == g * count + row_one, row, 0.0), axis=1, keepdims=True)

    def as_row(value):
        return jnp.sum(jnp.where(own_lane_one, value, 0.0), axis=0, keepdims=True)

    first = restrict([(residual[0], EAST), (residual[1], NORTH)])
    zmsg[0] = jnp.concatenate([first, jnp.zeros((4, lanes), f32)], axis=0)

    pl.semaphore_wait(barrier, narrow_count - 1 + wide_count - 1)

    def z_start(g):
        spread(zmsg.at[g], zbuf.at[g, narrow_at], z_send.at[g], z_recv.at[g], z_peer, narrow_count - 1)
        zbuf[g, narrow_at] = zmsg[g]

    msg_at = iota((msg_rows, 8 * narrow_count), 0)
    from_at = iota((msg_rows, 8 * narrow_count), 1)
    from_row = from_at & 7
    from_sub = from_at // 8
    verts = narrow_count + 1
    merge = (
        ((from_row == 0) & (msg_at == from_sub))
        | ((from_row == 1) & (msg_at == from_sub + 1))
        | ((from_row == 2) & (msg_at == from_sub + verts))
        | ((from_row == 3) & (msg_at == from_sub + verts + 1))
        | ((from_row == 4) & (msg_at == 2 * verts))
    ).astype(bf16)

    def w_start(g):
        drain(zbuf.at[g], narrow_count - 1, z_recv.at[g])
        high, low = split(zbuf[g].reshape(8 * narrow_count, lanes))
        wmsg[g] = mm(merge, high) + mm(merge, low)
        spread(wmsg.at[g], wbuf.at[g, wide_at], w_send.at[g], w_recv.at[g], w_peer, wide_count - 1)
        wbuf[g, wide_at] = wmsg[g]

    z_start(0)
    fore = [
        remote(fore_out.at[f], fore_in.at[f], fore_send.at[f], fore_recv.at[f], (east, north)[f])
        for f in range(2)
    ]
    for copy in fore:
        copy.start()
    spread(inverse, inverses.at[wide_at], inv_send, inv_recv, w_peer, wide_count - 1)
    inverses[wide_at] = inverse[...]

    for f in range(2):
        perm[f] = (iota((width, width), 0) == match[f : f + 1, :]).astype(bf16)
    low_wide = lax.axis_index("wide")
    vertex = [
        corners[low_wide, narrow_at],
        corners[low_wide, narrow_at + 1],
        corners[low_wide + 1, narrow_at],
        corners[low_wide + 1, narrow_at + 1],
    ]
    owner = [lax.div(v, capacity) for v in vertex]
    place_in = [v - b * capacity for v, b in zip(vertex, owner)]
    total_rows = wide_count * msg_rows
    for v in range(4):
        wanted = owner[v] * capacity + iota((order, total_rows), 0) // modes
        pick[v * order : (v + 1) * order, :] = (wanted == row_slots[...]).astype(f32).astype(bf16)
    pick[4 * order : 4 * order + 16, :] = (iota((16, total_rows), 1) % msg_rows == 2 * verts).astype(f32).astype(bf16)

    w_start(0)

    for f, copy in enumerate(fore):
        copy.wait_recv()
        got = mm(fore_in[f], perm[f])
        parts = []
        for base in (2 * count, 2 * count + 2 * modes):
            low_end = got[base : base + modes]
            high_end = got[base + modes : base + 2 * modes]
            if f == 0:
                parts += [low_end, high_end, nothing, nothing]
            else:
                parts += [low_end, nothing, high_end, nothing]
        set_face(
            WEST + f,
            got[0 : 2 * count].astype(bf16),
            jnp.concatenate(parts, axis=0).astype(bf16),
        )
    pltpu.make_async_copy(blocks, blocks, load_sem).wait()

    slot = [slots[0, d] for d in range(4)]
    base_out = []
    base_in = []
    for d in range(4):
        out = 0.0
        for s in range(4):
            out = out + mm(faces[s], blocks[slot[s], slot[d]])
        base_out.append(out[0:count] + out[count : 2 * count])
        high, low = split(
            out[2 * count : 2 * count + corner_rows]
            + out[2 * count + corner_rows : 2 * count + 2 * corner_rows]
        )
        lift[d, 0:corner_rows] = high
        lift[d, corner_rows : 2 * corner_rows] = high
        lift[d, 2 * corner_rows : 3 * corner_rows] = low
        lift[d, 3 * corner_rows :] = jnp.zeros((corner_rows, width), bf16)
        high = faces[d, 2 * count : 2 * count + corner_rows]
        lift[4 + d, 0:corner_rows] = high
        lift[4 + d, corner_rows : 2 * corner_rows] = high
        lift[4 + d, 2 * corner_rows : 3 * corner_rows] = faces[
            d, 2 * count + corner_rows : 2 * count + 2 * corner_rows
        ]
        lift[4 + d, 3 * corner_rows :] = jnp.zeros((corner_rows, width), bf16)
        base_in.append(
            faces[d, 0:count].astype(f32) + faces[d, count : 2 * count].astype(f32)
        )

    drain(inverses, wide_count - 1, inv_recv)
    for v in range(4):
        take = (iota((order, lanes), 0) == place_in[v] * modes + iota((order, lanes), 1) // count).astype(f32).astype(bf16)
        coef[v * order : (v + 1) * order, :] = fold(mm(halves(inverses[owner[v]]), take))

    tile = ((iota((2 * lanes, lanes), 0) % count) == (iota((2 * lanes, lanes), 1) % count)).astype(bf16)
    mode_lane = iota((4 * order, lanes), 1) // count == (iota((4 * order, lanes), 0) & (modes - 1))

    def gathered(g):
        drain(wbuf.at[g], wide_count - 1, w_recv.at[g])
        parts = jnp.concatenate(split(wbuf[g].reshape(total_rows, lanes)), axis=1)
        picked = mm(pick[...], parts)
        picked = picked[:, 0:lanes] + picked[:, lanes:]
        chosen = jnp.where(mode_lane, picked[0 : 4 * order], 0.0)
        tiled = mm(jnp.concatenate(split(chosen), axis=1), tile) * coef[...]
        rows = [
            jnp.sum(tiled[v * order : (v + 1) * order], axis=0, keepdims=True) for v in range(4)
        ]
        return jnp.concatenate(rows, axis=1), picked[4 * order : 4 * order + 1]

    shrink = (
        (iota((wide_lanes, 4 * corner_rows), 0) // count == (iota((wide_lanes, 4 * corner_rows), 1) & (corner_rows - 1)))
        & (iota((wide_lanes, 4 * corner_rows), 1) < 3 * corner_rows)
    ).astype(bf16)
    middle = iota((count, 4 * corner_rows), 1) // corner_rows == 1

    def lifted(correction):
        spread_out = jnp.where(own_lane, correction, 0.0)
        small = fold(mm(halves(spread_out), shrink))
        high, low = split(small)
        left = jnp.where(middle, low.astype(f32), high.astype(f32)).astype(bf16)
        return [mm(left, lift[d]) for d in range(8)]

    solved, _ = gathered(0)
    added = lifted(solved)
    direct = [base_in[d] + added[4 + d] for d in range(4)]
    product = [base_out[d] + added[d] for d in range(4)]

    def to_owner(k):
        copies = []
        for f in range(2):
            high, low = split(back_values[k][f])
            back_out[k, f] = mm_nt(high, perm[f]) + mm_nt(low, perm[f])
            copies.append(
                remote(
                    back_out.at[k, f],
                    back_in.at[k, f],
                    back_send.at[k, f],
                    back_recv.at[k, f],
                    (west, south)[f],
                )
            )
            copies[-1].start()
        return copies

    back_values = [None, None]
    coarse = restrict([(product[d], d) for d in range(4)])
    sums = pack(
        [
            inner([(residual[f], direct[f]) for f in range(2)]),
            inner([(direct[d], product[d]) for d in range(4)]),
        ]
    )
    zmsg[1] = jnp.concatenate([coarse, sums, jnp.zeros((3, lanes), f32)], axis=0)
    z_start(1)
    back_values[0] = product[2:]
    first_back = to_owner(0)
    applied = []
    for f in range(2):
        first_back[f].wait_recv()
        applied.append((product[f] + back_in[0, f]) * live[f])
        flux_out[f] = halves(applied[f] * weight[f])
    flux = [
        remote(flux_out.at[f], flux_in.at[f], flux_send.at[f], flux_recv.at[f], (east, north)[f])
        for f in range(2)
    ]
    for copy in flux:
        copy.start()
    w_start(1)
    own_flux = [flux_out[f] for f in range(2)]
    for f in range(2):
        flux[f].wait_recv()
        own_flux.append(mm(flux_in[f], perm[f]).astype(bf16))
    flux_product = []
    for d in range(4):
        out = 0.0
        for s in range(4):
            out = out + mm(own_flux[s], blocks[slot[s], slot[d]])
        flux_product.append(fold(out))

    change, sums = gathered(1)
    product_start = unpack(sums, 0)
    curvature = unpack(sums, 1)
    step = product_start / curvature
    step_row = as_row(step)
    solved = solved - jnp.concatenate([step_row] * 4, axis=1) * change
    added = lifted(solved)
    fresh = [
        base_in[d] - step * fold(own_flux[d].astype(f32)) + added[4 + d] for d in range(4)
    ]
    fresh_product = [base_out[d] - step * flux_product[d] + added[d] for d in range(4)]
    residual = [residual[f] - step * applied[f] for f in range(2)]
    zlast[...] = pack(
        [
            inner([(residual[f], fresh[f]) for f in range(2)]),
            inner([(fresh[d], fresh_product[d]) for d in range(4)]),
            inner([(fresh[f], applied[f]) for f in range(2)]),
        ]
    )
    spread(zlast, zlast_buf.at[narrow_at], z_send.at[2], z_recv.at[2], z_peer, narrow_count - 1)
    zlast_buf[narrow_at] = zlast[...]
    back_values[1] = fresh_product[2:]
    second_back = to_owner(1)
    drain(zlast_buf, narrow_count - 1, z_recv.at[2])
    wlast[...] = jnp.sum(zlast_buf[...], axis=0)
    spread(wlast, wlast_buf.at[wide_at], w_send.at[2], w_recv.at[2], w_peer, wide_count - 1)
    wlast_buf[wide_at] = wlast[...]
    fresh_applied = []
    for f in range(2):
        second_back[f].wait_recv()
        fresh_applied.append((fresh_product[f] + back_in[1, f]) * live[f])
    drain(wlast_buf, wide_count - 1, w_recv.at[2])
    sums = jnp.sum(wlast_buf[...], axis=0)
    product_fresh = unpack(sums, 0)
    ratio = product_fresh / product_start
    last_curvature = unpack(sums, 1) + 2.0 * ratio * unpack(sums, 2) + ratio * ratio * curvature
    last_step = product_fresh / last_curvature
    for f in range(2):
        sol_out[:, f, :] = step * direct[f] + last_step * (fresh[f] + ratio * direct[f])
        res_out[:, f, :] = residual[f] - last_step * (fresh_applied[f] + ratio * applied[f])

    for g in range(2):
        drain(zbuf.at[g], narrow_count - 1, z_send.at[g])
        drain(wbuf.at[g], wide_count - 1, w_send.at[g])
    drain(zlast_buf, narrow_count - 1, z_send.at[2])
    drain(wlast_buf, wide_count - 1, w_send.at[2])
    drain(inverses, wide_count - 1, inv_send)
    for copy in fore + flux + first_back + second_back:
        copy.wait_send()


def body(sources, schur, scaling, basis, inverse, sizes, match, slots, corners):
    wide_count = lax.axis_size("wide")
    narrow_count = lax.axis_size("narrow")
    count, width = sources.shape[2], sources.shape[4]
    modes = basis.shape[4]
    order = inverse.shape[1]
    lanes = modes * count
    verts = narrow_count + 1
    msg_rows = -(-(2 * verts + 1) // 8) * 8
    row_slots = jnp.pad(
        jnp.concatenate([corners[:-1], corners[1:]], axis=1),
        ((0, 0), (0, msg_rows - 2 * verts)),
        constant_values=-1,
    ).reshape(1, wide_count * msg_rows)
    vmem = pl.BlockSpec(memory_space=pltpu.VMEM)
    smem = pl.BlockSpec(memory_space=pltpu.SMEM)
    dma = pltpu.SemaphoreType.DMA
    out = jax.ShapeDtypeStruct((count, 2, width), f32)
    corner_rows = 4 * modes
    sol, res = pl.pallas_call(
        kernel,
        out_shape=(out, out),
        in_specs=[smem, smem, smem, vmem, pl.BlockSpec(memory_space=pltpu.HBM)] + [vmem] * 5,
        out_specs=(vmem, vmem),
        scratch_shapes=[
            pltpu.VMEM((4, 4, width, width), bf16),
            pltpu.VMEM((4, 2 * count + 2 * corner_rows, width), bf16),
            pltpu.VMEM((8, 4 * corner_rows, width), bf16),
            pltpu.VMEM((2, width, width), bf16),
            pltpu.VMEM((4 * order + 16, wide_count * msg_rows), bf16),
            pltpu.VMEM((4 * order, lanes), f32),
            pltpu.VMEM((wide_count, order, order), f32),
            pltpu.VMEM((2, 8, lanes), f32),
            pltpu.VMEM((2, narrow_count, 8, lanes), f32),
            pltpu.VMEM((2, msg_rows, lanes), f32),
            pltpu.VMEM((2, wide_count, msg_rows, lanes), f32),
            pltpu.VMEM((1, lanes), f32),
            pltpu.VMEM((narrow_count, 1, lanes), f32),
            pltpu.VMEM((1, lanes), f32),
            pltpu.VMEM((wide_count, 1, lanes), f32),
            pltpu.VMEM((2, 4 * count, width), bf16),
            pltpu.VMEM((2, 4 * count, width), bf16),
            pltpu.VMEM((2, 2 * count, width), bf16),
            pltpu.VMEM((2, 2 * count, width), bf16),
            pltpu.VMEM((2, 2, count, width), f32),
            pltpu.VMEM((2, 2, count, width), f32),
            dma,
            dma((3,)),
            dma((3,)),
            dma((3,)),
            dma((3,)),
            dma((2,)),
            dma((2,)),
            dma((2,)),
            dma((2,)),
            dma((2, 2)),
            dma((2, 2)),
            dma,
            dma,
        ],
        compiler_params=pltpu.CompilerParams(
            collective_id=0, has_side_effects=True, vmem_limit_bytes=48 << 20
        ),
    )(
        sizes[0],
        slots[0],
        corners,
        sources[0, 0],
        schur[0, 0],
        scaling[0, 0],
        basis[0, 0],
        inverse[0],
        match[0, 0],
        row_slots,
    )
    return sol[None, None], res[None, None]


def solution(mesh):
    placed = (
        P("wide", "narrow", None, None, None),
        P("wide", "narrow", None, None),
        P("wide", "narrow", None, None),
        P("wide", "narrow", None, None, None, None),
        P("wide", None, None),
        P("wide", "narrow", None),
        P("wide", "narrow", None, None),
        P("wide", "narrow", None),
        P(),
    )
    return jax.shard_map(
        body,
        mesh=mesh,
        in_specs=placed,
        out_specs=(P("wide", "narrow", None, None, None), P("wide", "narrow", None, None, None)),
        check_vma=False,
    )
```

time: 641 us -> 73.6 us (0.11)
  blocking collectives: 337 us -> 0 us
  waiting for transfers between devices: 224 us -> 0 us
  Pallas kernels: 0 us -> 64.3 us
  matrix products: 21.5 us -> 0 us
  starting transfers between devices: 17.5 us -> 0 us
  between operations: 15 us -> 0.65 us
  local copies, waits for them, and re-layouts: 18.9 us -> 8.22 us
    psum x5 -> x0, blocking collectives: 277 us -> none  [the longest x2 152 us: precondition(): lax.psum(jnp.sum(residual * precond, axis=(1, 2)), ('wide', 'narrow'))]
    unnamed x4 -> x0, waiting for transfers between devices: 217 us -> none
    pallas_call x0 -> x1, Pallas kernels: none -> 64.3 us  [body(): pl.pallas_call(kernel, out_shape=(out, out), in_specs=[smem, smem, smem,...]
    all_gather x2 -> x0, blocking collectives: 60.2 us -> none  [precondition(): lax.all_gather(solved.reshape(capacity, basis_count * nrhs_count), 'wide'...]
    dot_general x24 -> x0, matrix products: 21.5 us -> none  [the longest x2 11.3 us: body(): jnp.dot(slotted.reshape(nrhs_count, 4 * face_width), matrix, preferred_el...]
    ppermute x8 -> x0, starting transfers between devices: 17.5 us -> none  [shifted(): return lax.ppermute(block, axis, route)]
    dot_general x5 -> x0, local copies, waits for them, and re-layouts: 12.6 us -> none  [the longest x1 12.3 us: body(): jnp.dot(slotted.reshape(nrhs_count, 4 * face_width), matrix, preferred_el...]
    ppermute x8 -> x0, waiting for transfers between devices: 7.52 us -> none  [shifted(): return lax.ppermute(block, axis, route)]
  transfers between devices with their start and end apart: 10 -> 0, of which waited for: 8 -> 0; matrix products, arithmetic and copies ran while one was open for 2% -> 0% of each run, Pallas kernels for 0% -> 0%
where the time goes in v1:
time: 73.6 us; the launch traced here: 73.2 us
  Pallas kernels  64.3 us (87%)
  local copies, waits for them, and re-layouts  8.22 us (11%)
    pallas_call x1, Pallas kernels, body(): pl.pallas_call(kernel, out_shape=(out, out), in_specs=[smem, smem, smem,...  64.3 us
    unnamed x18, local copies, waits for them, and re-layouts  7.28 us

profile of v1, /device:TPU:1, one launch (start us, length us, event | category | flops | bytes accessed | tf_op | source)
XLA Modules:
  0.0 73.2 jit_solution(306384330546163350)
XLA Ops:
  0.6 0.8 %fusion = (s32[32,9]{0,1:T(8,128)S(1)}, s32[32,9]{0,1:T(8,128)S(1)}) fusion(s32[33,9]{0,1:T(8,128)} %param.17), kind=kLoop, calls=%fused_computation.1 | loop fusion | bytes 4608 | tf_op jit(solution)/shard_map/slice | solution.py:466
  1.5 0.1 copy.15
  1.6 0.1 reshape.7.row_slots
  1.7 0.8 %copy.14.corners = s32[33,9]{1,0:T(8,128)S(1)} copy(s32[33,9]{0,1:T(8,128)} %param.17) | data formatting | bytes 2376 | tf_op args[8]
  2.5 0.0 copy-start
  2.5 0.8 %copy-done = f32[1,1,16,2,512]{4,3,2,1,0:T(2,128)S(1)} copy-done((f32[1,1,16,2,512]{4,3,2,1,0:T(2,128)S(1)}, f32[1,1,16,2,512]{4,3,2,1,0:T(2,128)}, u32[]{:S(2)}) %copy-start) | copy-done | bytes 65560
  3.3 0.0 copy-start.1
  3.3 0.8 %copy-done.1 = f32[1,1,2,2,8,512]{5,4,3,2,1,0:T(8,128)S(1)} copy-done((f32[1,1,2,2,8,512]{5,4,3,2,1,0:T(8,128)S(1)}, f32[1,1,2,2,8,512]{5,4,3,2,1,0:T(8,128)}, u32[]{:S(2)}) %copy-start.1) | copy-done | bytes 65560
  4.1 0.0 copy-start.2
  4.1 0.8 %copy-done.2 = f32[1,80,80]{2,1,0:T(8,128)S(1)} copy-done((f32[1,80,80]{2,1,0:T(8,128)S(1)}, f32[1,80,80]{2,1,0:T(8,128)}, u32[]{:S(2)}) %copy-start.2) | copy-done | bytes 25624
  4.9 0.0 copy-start.3
  4.9 0.7 copy-done.3
  5.6 0.0 copy-start.4
  5.6 0.7 copy-done.4
  6.3 0.0 copy-start.5
  6.3 0.7 copy-done.5
  7.0 0.0 copy-start.6
  7.0 0.7 copy-done.6
  7.6 64.3 %shard_map.104 = (f32[16,2,512]{2,1,0:T(2,128)S(1)}, f32[16,2,512]{2,1,0:T(2,128)S(1)}) custom-call(s32[1,2]{1,0:T(1,128)S(1)} %bitcast.17, s32[1,4]{1,0:T(1,128)S(1)} %bitcast.18, s32[33,9]{1,0:T(8,128)S(1)} %copy.14.corners, f32[16,2,512]{2,1,0:T(2,128)S(1)} %bitcast.10, bf16[2048,2048]{1,0:T(8,128)(2,1)} %bitcast.19, f32[2,512]{1,0:T(2,128)S(1)} %bitcast.15, ...), custom_call_target="tpu_custom_call" | custom-call | tf_op jit(solution)/shard_map/pallas_call | solution.py:475
  71.9 0.6 copy.18
  72.6 0.6 copy.19
  (2 shorter events, 0.0 us)
Async XLA Ops:
  2.5 0.8 %copy-start = (f32[1,1,16,2,512]{4,3,2,1,0:T(2,128)S(1)}, f32[1,1,16,2,512]{4,3,2,1,0:T(2,128)}, u32[]{:S(2)}) copy-start(f32[1,1,16,2,512]{4,3,2,1,0:T(2,128)} %param.9) | copy-start | bytes 196612
  3.3 0.8 %copy-start.1 = (f32[1,1,2,2,8,512]{5,4,3,2,1,0:T(8,128)S(1)}, f32[1,1,2,2,8,512]{5,4,3,2,1,0:T(8,128)}, u32[]{:S(2)}) copy-start(f32[1,1,2,2,8,512]{5,4,3,2,1,0:T(8,128)} %param.12) | copy-start | bytes 196612
  4.1 0.8 %copy-start.2 = (f32[1,80,80]{2,1,0:T(8,128)S(1)}, f32[1,80,80]{2,1,0:T(8,128)}, u32[]{:S(2)}) copy-start(f32[1,80,80]{2,1,0:T(8,128)} %param.13) | copy-start | bytes 76804
  4.9 0.7 copy-start.3
  5.6 0.7 copy-start.4
  6.3 0.7 copy-start.5
  7.0 0.7 copy-start.6

commit v2 on v1

--- a/solution.py
+++ b/solution.py
@@ -39,24 +39,33 @@
 
 
 def kernel(
-    sizes,
-    slots,
-    corners,
+    src_hbm,
+    schur,
+    scaling_hbm,
+    basis_hbm,
+    inverse_hbm,
+    sizes_hbm,
+    match_hbm,
+    slots_hbm,
+    corners_hbm,
+    sol_out,
+    res_out,
     src,
-    schur,
     scaling,
     basis,
     inverse,
     match,
-    row_slots,
-    sol_out,
-    res_out,
+    table,
+    sizes,
+    slots,
+    corners,
     blocks,
     faces,
     lift,
     perm,
     pick,
     coef,
+    packed,
     inverses,
     zmsg,
     zbuf,
@@ -72,6 +81,7 @@
     flux_in,
     back_out,
     back_in,
+    in_sem,
     load_sem,
     z_send,
     z_recv,
@@ -93,14 +103,26 @@
     count = src.shape[0]
     width = src.shape[2]
     order = inverse.shape[0]
+    half = order // 2
     modes = basis.shape[2]
     capacity = order // modes
     lanes = modes * count
     corner_rows = 4 * modes
     msg_rows = wmsg.shape[1]
+    verts = narrow_count + 1
+
+    chips = wide_count // 2
+    chip_at = wide_at // 2
+    core_at = lax.rem(wide_at, 2)
+    team = 2 * narrow_count
+    rank = 2 * narrow_at + core_at
 
     def z_peer(k):
-        return (wide_at, lax.rem(narrow_at + 1 + k, narrow_count))
+        other = lax.rem(rank + 1 + k, team)
+        return (2 * chip_at + lax.rem(other, 2), other // 2)
+
+    def c_peer(k):
+        return (2 * lax.rem(chip_at + 1 + k, chips) + core_at, narrow_at)
 
     def w_peer(k):
         return (lax.rem(wide_at + 1 + k, wide_count), narrow_at)
@@ -110,6 +132,25 @@
     north = (wide_at, lax.rem(narrow_at + 1, narrow_count))
     south = (wide_at, lax.rem(narrow_at + narrow_count - 1, narrow_count))
 
+    loads = [
+        pltpu.make_async_copy(a, b, in_sem.at[i])
+        for i, (a, b) in enumerate(
+            [
+                (sizes_hbm, sizes),
+                (src_hbm, src),
+                (basis_hbm, basis),
+                (scaling_hbm, scaling),
+                (inverse_hbm, inverse),
+                (match_hbm, match),
+                (slots_hbm, slots),
+                (corners_hbm, corners),
+                (corners_hbm, table),
+            ]
+        )
+    ]
+    for copy in loads:
+        copy.start()
+
     barrier = pltpu.get_barrier_semaphore()
 
     def greet(peer, number):
@@ -119,7 +160,7 @@
 
         lax.fori_loop(0, number, one, 0)
 
-    greet(z_peer, narrow_count - 1)
+    greet(z_peer, team - 1)
     greet(w_peer, wide_count - 1)
 
     for s in range(4):
@@ -130,22 +171,37 @@
                 load_sem,
             ).start()
 
+    pending = {}
+
     def remote(a, b, send, recv, device):
         return pltpu.make_async_remote_copy(
             src_ref=a, dst_ref=b, send_sem=send, recv_sem=recv, device_id=device, device_id_type=MESH
         )
 
-    def spread(a, b, send, recv, peer, number):
-        def one(k, carry):
-            remote(a, b, send, recv, peer(k)).start()
-            return carry
-
-        lax.fori_loop(0, number, one, 0)
-
-    def drain(ref, number, sem):
+    def wait_bytes(ref, number, sem):
         part = ref.at[pl.ds(0, number)]
         pltpu.make_async_copy(part, part, sem).wait()
 
+    def spread(name, a, buf, at, send, recv, peer, number):
+        def one(k, carry):
+            remote(a, buf.at[at], send, recv, peer(k)).start()
+            return carry
+
+        lax.fori_loop(0, number, one, 0)
+        pending["send " + name] = lambda: wait_bytes(buf, number, send)
+        pending[name] = lambda: wait_bytes(buf, number, recv)
+
+    def single(name, a, b, send, recv, device):
+        copy = remote(a, b, send, recv, device)
+        copy.start()
+        pending["send " + name] = copy.wait_send
+        pending[name] = copy.wait_recv
+
+    def arrive(name):
+        pending.pop(name)()
+
+    for copy in loads[:4]:
+        copy.wait()
     place = iota((1, width), 1)
     live = [(place < sizes[0, f]).astype(f32) for f in range(2)]
     weight = [scaling[f : f + 1, :] * live[f] for f in range(2)]
@@ -174,7 +230,7 @@
     )
 
     wide_lanes = 4 * lanes
-    grow = ((iota((2 * corner_rows, wide_lanes), 0) & (corner_rows - 1)) == iota((2 * corner_rows, wide_lanes), 1) // count).astype(bf16)
+    grow = ((iota((2 * corner_rows, wide_lanes), 0) & (corner_rows - 1)) == iota((2 * corner_rows, wide_lanes), 1) // count).astype(f32).astype(bf16)
     own_lane = iota((count, wide_lanes), 1) % count == iota((count, wide_lanes), 0)
     own_lane_one = own_lane[:, 0:lanes]
 
@@ -212,63 +268,77 @@
     first = restrict([(residual[0], EAST), (residual[1], NORTH)])
     zmsg[0] = jnp.concatenate([first, jnp.zeros((4, lanes), f32)], axis=0)
 
-    pl.semaphore_wait(barrier, narrow_count - 1 + wide_count - 1)
+    loads[4].wait()
+    from_lane = iota((order, lanes), 0)
+    to_lane = iota((order, lanes), 1)
+    top = ((from_lane == to_lane) & (to_lane < order)).astype(f32).astype(bf16)
+    corner = ((from_lane == to_lane - half) & (to_lane >= order)).astype(f32).astype(bf16)
+    packed[...] = fold(mm(halves(inverse[0:half, :]), top)) + fold(
+        mm(halves(inverse[half:order, :]), corner)
+    )
+
+    pl.semaphore_wait(barrier, team - 1 + wide_count - 1)
 
     def z_start(g):
-        spread(zmsg.at[g], zbuf.at[g, narrow_at], z_send.at[g], z_recv.at[g], z_peer, narrow_count - 1)
-        zbuf[g, narrow_at] = zmsg[g]
-
-    msg_at = iota((msg_rows, 8 * narrow_count), 0)
-    from_at = iota((msg_rows, 8 * narrow_count), 1)
+        spread(f"z{g}", zmsg.at[g], zbuf.at[g], rank, z_send.at[g], z_recv.at[g], z_peer, team - 1)
+        zbuf[g, rank] = zmsg[g]
+
+    msg_at = iota((msg_rows, 8 * team), 0)
+    from_at = iota((msg_rows, 8 * team), 1)
     from_row = from_at & 7
-    from_sub = from_at // 8
-    verts = narrow_count + 1
-    merge = (
-        ((from_row == 0) & (msg_at == from_sub))
-        | ((from_row == 1) & (msg_at == from_sub + 1))
-        | ((from_row == 2) & (msg_at == from_sub + verts))
-        | ((from_row == 3) & (msg_at == from_sub + verts + 1))
-        | ((from_row == 4) & (msg_at == 2 * verts))
-    ).astype(bf16)
+    from_col = (from_at // 8) & 1
+    from_sub = from_at // 16
+    goes = (from_col + from_row // 2) * verts + from_sub + (from_row & 1)
+    goes = jnp.where(from_row < 4, goes, jnp.where(from_row == 4, 3 * verts, -1))
+    merge = (msg_at == goes).astype(f32).astype(bf16)
 
     def w_start(g):
-        drain(zbuf.at[g], narrow_count - 1, z_recv.at[g])
-        high, low = split(zbuf[g].reshape(8 * narrow_count, lanes))
+        arrive(f"z{g}")
+        high, low = split(zbuf[g].reshape(8 * team, lanes))
         wmsg[g] = mm(merge, high) + mm(merge, low)
-        spread(wmsg.at[g], wbuf.at[g, wide_at], w_send.at[g], w_recv.at[g], w_peer, wide_count - 1)
-        wbuf[g, wide_at] = wmsg[g]
+        spread(f"w{g}", wmsg.at[g], wbuf.at[g], chip_at, w_send.at[g], w_recv.at[g], c_peer, chips - 1)
+        wbuf[g, chip_at] = wmsg[g]
 
     z_start(0)
-    fore = [
-        remote(fore_out.at[f], fore_in.at[f], fore_send.at[f], fore_recv.at[f], (east, north)[f])
-        for f in range(2)
-    ]
-    for copy in fore:
-        copy.start()
-    spread(inverse, inverses.at[wide_at], inv_send, inv_recv, w_peer, wide_count - 1)
-    inverses[wide_at] = inverse[...]
-
-    for f in range(2):
-        perm[f] = (iota((width, width), 0) == match[f : f + 1, :]).astype(bf16)
-    low_wide = lax.axis_index("wide")
+    for f in range(2):
+        single(f"fore{f}", fore_out.at[f], fore_in.at[f], fore_send.at[f], fore_recv.at[f], (east, north)[f])
+    spread("inv", packed, inverses, wide_at, inv_send, inv_recv, w_peer, wide_count - 1)
+    inverses[wide_at] = packed[...]
+
+    for copy in loads[5:]:
+        copy.wait()
+    for f in range(2):
+        perm[f] = (iota((width, width), 0) == match[f : f + 1, :]).astype(f32).astype(bf16)
     vertex = [
-        corners[low_wide, narrow_at],
-        corners[low_wide, narrow_at + 1],
-        corners[low_wide + 1, narrow_at],
-        corners[low_wide + 1, narrow_at + 1],
+        corners[wide_at, narrow_at],
+        corners[wide_at, narrow_at + 1],
+        corners[wide_at + 1, narrow_at],
+        corners[wide_at + 1, narrow_at + 1],
     ]
     owner = [lax.div(v, capacity) for v in vertex]
     place_in = [v - b * capacity for v, b in zip(vertex, owner)]
-    total_rows = wide_count * msg_rows
+    total_rows = chips * msg_rows
+    row_at = iota((wide_count + 1, total_rows), 1)
+    in_msg = row_at % msg_rows
+    reach = (
+        (iota((wide_count + 1, total_rows), 0) == 2 * (row_at // msg_rows) + in_msg // verts) & (in_msg < 3 * verts)
+    ).astype(f32).astype(bf16)
+    same = (iota((16, verts), 0) == iota((16, verts), 1)).astype(f32).astype(bf16)
+    each = 0.0
+    for part in split(table[...].astype(f32)):
+        each = each + mm(mm_nt(same, part).astype(bf16), reach)
+    row_at = iota((16, total_rows), 1) % msg_rows
+    row_slots = jnp.sum(jnp.where(iota((16, total_rows), 0) == row_at % verts, each, 0.0), axis=0, keepdims=True)
+    row_slots = jnp.where(iota((1, total_rows), 1) % msg_rows < 3 * verts, row_slots, -1.0)
     for v in range(4):
-        wanted = owner[v] * capacity + iota((order, total_rows), 0) // modes
-        pick[v * order : (v + 1) * order, :] = (wanted == row_slots[...]).astype(f32).astype(bf16)
-    pick[4 * order : 4 * order + 16, :] = (iota((16, total_rows), 1) % msg_rows == 2 * verts).astype(f32).astype(bf16)
+        wanted = (owner[v] * capacity + iota((order, 1), 0) // modes).astype(f32)
+        pick[v * order : (v + 1) * order, :] = (wanted == row_slots).astype(f32).astype(bf16)
+    pick[4 * order : 4 * order + 16, :] = (iota((16, total_rows), 1) % msg_rows == 3 * verts).astype(f32).astype(bf16)
 
     w_start(0)
 
-    for f, copy in enumerate(fore):
-        copy.wait_recv()
+    for f in range(2):
+        arrive(f"fore{f}")
         got = mm(fore_in[f], perm[f])
         parts = []
         for base in (2 * count, 2 * count + 2 * modes):
@@ -312,16 +382,23 @@
             faces[d, 0:count].astype(f32) + faces[d, count : 2 * count].astype(f32)
         )
 
-    drain(inverses, wide_count - 1, inv_recv)
+    arrive("inv")
     for v in range(4):
-        take = (iota((order, lanes), 0) == place_in[v] * modes + iota((order, lanes), 1) // count).astype(f32).astype(bf16)
-        coef[v * order : (v + 1) * order, :] = fold(mm(halves(inverses[owner[v]]), take))
-
-    tile = ((iota((2 * lanes, lanes), 0) % count) == (iota((2 * lanes, lanes), 1) % count)).astype(bf16)
+        column = place_in[v] * modes + iota((lanes, 2 * lanes), 1) % lanes // count
+        column = jnp.where(iota((lanes, 2 * lanes), 1) < lanes, column, column + half)
+        take = ((iota((lanes, 2 * lanes), 0) == column) & (place_in[v] * modes >= half)).astype(f32).astype(bf16)
+        across = ((iota((order, lanes), 0) % half == place_in[v] * modes + iota((order, lanes), 1) // count) & (place_in[v] * modes < half)).astype(f32).astype(bf16)
+        mine = halves(inverses[owner[v]])
+        right = fold(mm(mine, take))
+        left = lax.dot_general(mine, across, (((0,), (0,)), ((), ())), preferred_element_type=f32)
+        coef[v * order : v * order + half, :] = left[0:half] + right[:, 0:lanes]
+        coef[v * order + half : (v + 1) * order, :] = left[half:order] + right[:, lanes:]
+
+    tile = ((iota((2 * lanes, lanes), 0) % count) == (iota((2 * lanes, lanes), 1) % count)).astype(f32).astype(bf16)
     mode_lane = iota((4 * order, lanes), 1) // count == (iota((4 * order, lanes), 0) & (modes - 1))
 
     def gathered(g):
-        drain(wbuf.at[g], wide_count - 1, w_recv.at[g])
+        arrive(f"w{g}")
         parts = jnp.concatenate(split(wbuf[g].reshape(total_rows, lanes)), axis=1)
         picked = mm(pick[...], parts)
         picked = picked[:, 0:lanes] + picked[:, lanes:]
@@ -335,7 +412,7 @@
     shrink = (
         (iota((wide_lanes, 4 * corner_rows), 0) // count == (iota((wide_lanes, 4 * corner_rows), 1) & (corner_rows - 1)))
         & (iota((wide_lanes, 4 * corner_rows), 1) < 3 * corner_rows)
-    ).astype(bf16)
+    ).astype(f32).astype(bf16)
     middle = iota((count, 4 * corner_rows), 1) // corner_rows == 1
 
     def lifted(correction):
@@ -350,24 +427,19 @@
     direct = [base_in[d] + added[4 + d] for d in range(4)]
     product = [base_out[d] + added[d] for d in range(4)]
 
-    def to_owner(k):
-        copies = []
+    def to_owner(k, values):
         for f in range(2):
-            high, low = split(back_values[k][f])
+            high, low = split(values[f])
             back_out[k, f] = mm_nt(high, perm[f]) + mm_nt(low, perm[f])
-            copies.append(
-                remote(
-                    back_out.at[k, f],
-                    back_in.at[k, f],
-                    back_send.at[k, f],
-                    back_recv.at[k, f],
-                    (west, south)[f],
-                )
+            single(
+                f"back{k}{f}",
+                back_out.at[k, f],
+                back_in.at[k, f],
+                back_send.at[k, f],
+                back_recv.at[k, f],
+                (west, south)[f],
             )
-            copies[-1].start()
-        return copies
-
-    back_values = [None, None]
+
     coarse = restrict([(product[d], d) for d in range(4)])
     sums = pack(
         [
@@ -377,23 +449,17 @@
     )
     zmsg[1] = jnp.concatenate([coarse, sums, jnp.zeros((3, lanes), f32)], axis=0)
     z_start(1)
-    back_values[0] = product[2:]
-    first_back = to_owner(0)
+    to_owner(0, product[2:])
     applied = []
     for f in range(2):
-        first_back[f].wait_recv()
+        arrive(f"back0{f}")
         applied.append((product[f] + back_in[0, f]) * live[f])
         flux_out[f] = halves(applied[f] * weight[f])
-    flux = [
-        remote(flux_out.at[f], flux_in.at[f], flux_send.at[f], flux_recv.at[f], (east, north)[f])
-        for f in range(2)
-    ]
-    for copy in flux:
-        copy.start()
+        single(f"flux{f}", flux_out.at[f], flux_in.at[f], flux_send.at[f], flux_recv.at[f], (east, north)[f])
     w_start(1)
     own_flux = [flux_out[f] for f in range(2)]
     for f in range(2):
-        flux[f].wait_recv()
+        arrive(f"flux{f}")
         own_flux.append(mm(flux_in[f], perm[f]).astype(bf16))
     flux_product = []
     for d in range(4):
@@ -421,19 +487,18 @@
             inner([(fresh[f], applied[f]) for f in range(2)]),
         ]
     )
-    spread(zlast, zlast_buf.at[narrow_at], z_send.at[2], z_recv.at[2], z_peer, narrow_count - 1)
-    zlast_buf[narrow_at] = zlast[...]
-    back_values[1] = fresh_product[2:]
-    second_back = to_owner(1)
-    drain(zlast_buf, narrow_count - 1, z_recv.at[2])
+    spread("zlast", zlast, zlast_buf, rank, z_send.at[2], z_recv.at[2], z_peer, team - 1)
+    zlast_buf[rank] = zlast[...]
+    to_owner(1, fresh_product[2:])
+    arrive("zlast")
     wlast[...] = jnp.sum(zlast_buf[...], axis=0)
-    spread(wlast, wlast_buf.at[wide_at], w_send.at[2], w_recv.at[2], w_peer, wide_count - 1)
-    wlast_buf[wide_at] = wlast[...]
+    spread("wlast", wlast, wlast_buf, chip_at, w_send.at[2], w_recv.at[2], c_peer, chips - 1)
+    wlast_buf[chip_at] = wlast[...]
     fresh_applied = []
     for f in range(2):
-        second_back[f].wait_recv()
+        arrive(f"back1{f}")
         fresh_applied.append((fresh_product[f] + back_in[1, f]) * live[f])
-    drain(wlast_buf, wide_count - 1, w_recv.at[2])
+    arrive("wlast")
     sums = jnp.sum(wlast_buf[...], axis=0)
     product_fresh = unpack(sums, 0)
     ratio = product_fresh / product_start
@@ -443,14 +508,8 @@
         sol_out[:, f, :] = step * direct[f] + last_step * (fresh[f] + ratio * direct[f])
         res_out[:, f, :] = residual[f] - last_step * (fresh_applied[f] + ratio * applied[f])
 
-    for g in range(2):
-        drain(zbuf.at[g], narrow_count - 1, z_send.at[g])
-        drain(wbuf.at[g], wide_count - 1, w_send.at[g])
-    drain(zlast_buf, narrow_count - 1, z_send.at[2])
-    drain(wlast_buf, wide_count - 1, w_send.at[2])
-    drain(inverses, wide_count - 1, inv_send)
-    for copy in fore + flux + first_back + second_back:
-        copy.wait_send()
+    for wait in list(pending.values()):
+        wait()
 
 
 def body(sources, schur, scaling, basis, inverse, sizes, match, slots, corners):
@@ -461,44 +520,52 @@
     order = inverse.shape[1]
     lanes = modes * count
     verts = narrow_count + 1
-    msg_rows = -(-(2 * verts + 1) // 8) * 8
-    row_slots = jnp.pad(
-        jnp.concatenate([corners[:-1], corners[1:]], axis=1),
-        ((0, 0), (0, msg_rows - 2 * verts)),
-        constant_values=-1,
-    ).reshape(1, wide_count * msg_rows)
+    team = 2 * narrow_count
+    chips = wide_count // 2
+    msg_rows = -(-(3 * verts + 1) // 8) * 8
     vmem = pl.BlockSpec(memory_space=pltpu.VMEM)
-    smem = pl.BlockSpec(memory_space=pltpu.SMEM)
+    hbm = pl.BlockSpec(memory_space=pltpu.HBM)
     dma = pltpu.SemaphoreType.DMA
     out = jax.ShapeDtypeStruct((count, 2, width), f32)
     corner_rows = 4 * modes
     sol, res = pl.pallas_call(
         kernel,
         out_shape=(out, out),
-        in_specs=[smem, smem, smem, vmem, pl.BlockSpec(memory_space=pltpu.HBM)] + [vmem] * 5,
+        in_specs=[hbm] * 9,
         out_specs=(vmem, vmem),
         scratch_shapes=[
+            pltpu.VMEM((count, 2, width), f32),
+            pltpu.VMEM((2, width), f32),
+            pltpu.VMEM((2, 2, modes, width), f32),
+            pltpu.VMEM((order, order), f32),
+            pltpu.VMEM((2, width), jnp.int32),
+            pltpu.VMEM((wide_count + 1, verts), jnp.int32),
+            pltpu.SMEM((1, 2), jnp.int32),
+            pltpu.SMEM((1, 4), jnp.int32),
+            pltpu.SMEM((wide_count + 1, verts), jnp.int32),
             pltpu.VMEM((4, 4, width, width), bf16),
             pltpu.VMEM((4, 2 * count + 2 * corner_rows, width), bf16),
             pltpu.VMEM((8, 4 * corner_rows, width), bf16),
             pltpu.VMEM((2, width, width), bf16),
-            pltpu.VMEM((4 * order + 16, wide_count * msg_rows), bf16),
+            pltpu.VMEM((4 * order + 16, chips * msg_rows), bf16),
             pltpu.VMEM((4 * order, lanes), f32),
-            pltpu.VMEM((wide_count, order, order), f32),
+            pltpu.VMEM((order // 2, lanes), f32),
+            pltpu.VMEM((wide_count, order // 2, lanes), f32),
             pltpu.VMEM((2, 8, lanes), f32),
-            pltpu.VMEM((2, narrow_count, 8, lanes), f32),
+            pltpu.VMEM((2, team, 8, lanes), f32),
             pltpu.VMEM((2, msg_rows, lanes), f32),
-            pltpu.VMEM((2, wide_count, msg_rows, lanes), f32),
+            pltpu.VMEM((2, chips, msg_rows, lanes), f32),
             pltpu.VMEM((1, lanes), f32),
-            pltpu.VMEM((narrow_count, 1, lanes), f32),
+            pltpu.VMEM((team, 1, lanes), f32),
             pltpu.VMEM((1, lanes), f32),
-            pltpu.VMEM((wide_count, 1, lanes), f32),
+            pltpu.VMEM((chips, 1, lanes), f32),
             pltpu.VMEM((2, 4 * count, width), bf16),
             pltpu.VMEM((2, 4 * count, width), bf16),
             pltpu.VMEM((2, 2 * count, width), bf16),
             pltpu.VMEM((2, 2 * count, width), bf16),
             pltpu.VMEM((2, 2, count, width), f32),
             pltpu.VMEM((2, 2, count, width), f32),
+            dma((9,)),
             dma,
             dma((3,)),
             dma((3,)),
@@ -517,16 +584,15 @@
             collective_id=0, has_side_effects=True, vmem_limit_bytes=48 << 20
         ),
     )(
-        sizes[0],
-        slots[0],
-        corners,
         sources[0, 0],
         schur[0, 0],
         scaling[0, 0],
         basis[0, 0],
         inverse[0],
+        sizes[0],
         match[0, 0],
-        row_slots,
+        slots[0],
+        corners,
     )
     return sol[None, None], res[None, None]
 

time: 73.6 us -> 57.8 us (0.79)
  Pallas kernels: 64.3 us -> 49.6 us
  local copies, waits for them, and re-layouts: 8.22 us -> 7.19 us
    pallas_call x1, Pallas kernels: 64.3 us -> 49.6 us  [body(): pl.pallas_call(kernel, out_shape=(out, out), in_specs=[hbm] * 9, out_spec...]
    slice x1 -> x0, local copies, waits for them, and re-layouts: 0.85 us -> none  [body(): corners[:-1]]
    unnamed x18 -> x17, local copies, waits for them, and re-layouts: 7.28 us -> 7.19 us
where the time goes in v2:
time: 57.8 us; the launch traced here: 57.5 us
  Pallas kernels  49.6 us (86%)
  local copies, waits for them, and re-layouts  7.19 us (12%)
  between operations  0.65 us (1%)
    pallas_call x1, Pallas kernels, body(): pl.pallas_call(kernel, out_shape=(out, out), in_specs=[hbm] * 9, out_spec...  49.6 us
    unnamed x17, local copies, waits for them, and re-layouts  7.19 us

profile of v2, /device:TPU:1, one launch (start us, length us, event | category | flops | bytes accessed | tf_op | source)
XLA Modules:
  0.0 57.5 jit_solution(15585356446040401397)
XLA Ops:
  0.6 0.8 %copy.11.corners_hbm = s32[33,9]{1,0:T(8,128)S(1)} copy(s32[33,9]{0,1:T(8,128)} %param.17) | data formatting | bytes 2376 | tf_op args[8]
  1.4 0.0 copy-start
  1.4 0.8 %copy-done = f32[1,1,16,2,512]{4,3,2,1,0:T(2,128)S(1)} copy-done((f32[1,1,16,2,512]{4,3,2,1,0:T(2,128)S(1)}, f32[1,1,16,2,512]{4,3,2,1,0:T(2,128)}, u32[]{:S(2)}) %copy-start) | copy-done | bytes 65560
  2.3 0.0 copy-start.1
  2.3 0.8 %copy-done.1 = f32[1,1,2,2,8,512]{5,4,3,2,1,0:T(8,128)S(1)} copy-done((f32[1,1,2,2,8,512]{5,4,3,2,1,0:T(8,128)S(1)}, f32[1,1,2,2,8,512]{5,4,3,2,1,0:T(8,128)}, u32[]{:S(2)}) %copy-start.1) | copy-done | bytes 65560
  3.1 0.0 copy-start.2
  3.1 0.8 %copy-done.2 = f32[1,80,80]{2,1,0:T(8,128)S(1)} copy-done((f32[1,80,80]{2,1,0:T(8,128)S(1)}, f32[1,80,80]{2,1,0:T(8,128)}, u32[]{:S(2)}) %copy-start.2) | copy-done | bytes 25624
  3.9 0.0 copy-start.3
  3.9 0.7 %copy-done.3 = f32[1,1,2,512]{3,2,1,0:T(2,128)S(1)} copy-done((f32[1,1,2,512]{3,2,1,0:T(2,128)S(1)}, f32[1,1,2,512]{3,2,1,0:T(2,128)}, u32[]{:S(2)}) %copy-start.3) | copy-done | bytes 4120
  4.6 0.0 copy-start.4
  4.6 0.7 %copy-done.4 = s32[1,1,2,512]{3,2,1,0:T(2,128)S(1)} copy-done((s32[1,1,2,512]{3,2,1,0:T(2,128)S(1)}, s32[1,1,2,512]{3,2,1,0:T(2,128)}, u32[]{:S(2)}) %copy-start.4) | copy-done | bytes 4120
  5.3 0.0 copy-start.5
  5.3 0.7 %copy-done.5 = s32[1,1,2]{2,1,0:T(1,128)S(1)} copy-done((s32[1,1,2]{2,1,0:T(1,128)S(1)}, s32[1,1,2]{2,1,0:T(1,128)}, u32[]{:S(2)}) %copy-start.5) | copy-done | bytes 32
  5.9 0.0 copy-start.6
  5.9 0.7 %copy-done.6 = s32[1,1,4]{2,1,0:T(1,128)S(1)} copy-done((s32[1,1,4]{2,1,0:T(1,128)S(1)}, s32[1,1,4]{2,1,0:T(1,128)}, u32[]{:S(2)}) %copy-start.6) | copy-done | bytes 40
  6.6 49.6 %shard_map.104 = (f32[16,2,512]{2,1,0:T(2,128)S(1)}, f32[16,2,512]{2,1,0:T(2,128)S(1)}) custom-call(f32[16,2,512]{2,1,0:T(2,128)S(1)} %bitcast.10, bf16[2048,2048]{1,0:T(8,128)(2,1)} %bitcast.19, f32[2,512]{1,0:T(2,128)S(1)} %bitcast.15, f32[2,2,8,512]{3,2,1,0:T(8,128)S(1)} %bitcast.11, f32[80,80]{1,0:T(8,128)S(1)} %bitcast.14, s32[1,2]{1,0:T(1,128)S(1)} %bitcast.17, ...), custom_call_target="tpu_custom_call" | custom-call | tf_op jit(solution)/shard_map/pallas_call | solution.py:531
  56.2 0.6 %copy.14 = f32[1,1,16,2,512]{4,3,2,1,0:T(2,128)} copy(f32[1,1,16,2,512]{4,3,2,1,0:T(2,128)S(1)} %bitcast.13) | data formatting | bytes 131072
  56.8 0.6 %copy.15 = f32[1,1,16,2,512]{4,3,2,1,0:T(2,128)} copy(f32[1,1,16,2,512]{4,3,2,1,0:T(2,128)S(1)} %bitcast.12) | data formatting | bytes 131072
Async XLA Ops:
  1.4 0.8 %copy-start = (f32[1,1,16,2,512]{4,3,2,1,0:T(2,128)S(1)}, f32[1,1,16,2,512]{4,3,2,1,0:T(2,128)}, u32[]{:S(2)}) copy-start(f32[1,1,16,2,512]{4,3,2,1,0:T(2,128)} %param.9) | copy-start | bytes 196612
  2.3 0.8 %copy-start.1 = (f32[1,1,2,2,8,512]{5,4,3,2,1,0:T(8,128)S(1)}, f32[1,1,2,2,8,512]{5,4,3,2,1,0:T(8,128)}, u32[]{:S(2)}) copy-start(f32[1,1,2,2,8,512]{5,4,3,2,1,0:T(8,128)} %param.12) | copy-start | bytes 196612
  3.1 0.8 %copy-start.2 = (f32[1,80,80]{2,1,0:T(8,128)S(1)}, f32[1,80,80]{2,1,0:T(8,128)}, u32[]{:S(2)}) copy-start(f32[1,80,80]{2,1,0:T(8,128)} %param.13) | copy-start | bytes 76804
  3.9 0.7 %copy-start.3 = (f32[1,1,2,512]{3,2,1,0:T(2,128)S(1)}, f32[1,1,2,512]{3,2,1,0:T(2,128)}, u32[]{:S(2)}) copy-start(f32[1,1,2,512]{3,2,1,0:T(2,128)} %param.11) | copy-start | bytes 12292
  4.6 0.7 %copy-start.4 = (s32[1,1,2,512]{3,2,1,0:T(2,128)S(1)}, s32[1,1,2,512]{3,2,1,0:T(2,128)}, u32[]{:S(2)}) copy-start(s32[1,1,2,512]{3,2,1,0:T(2,128)} %param.15) | copy-start | bytes 12292
  5.3 0.7 %copy-start.5 = (s32[1,1,2]{2,1,0:T(1,128)S(1)}, s32[1,1,2]{2,1,0:T(1,128)}, u32[]{:S(2)}) copy-start(s32[1,1,2]{2,1,0:T(1,128)} %param.14) | copy-start | bytes 28
  5.9 0.7 %copy-start.6 = (s32[1,1,4]{2,1,0:T(1,128)S(1)}, s32[1,1,4]{2,1,0:T(1,128)}, u32[]{:S(2)}) copy-start(s32[1,1,4]{2,1,0:T(1,128)} %param.16) | copy-start | bytes 52

commit v3 on v2

--- a/solution.py
+++ b/solution.py
@@ -14,6 +14,18 @@
 
 def iota(shape, dim):
     return lax.broadcasted_iota(jnp.int32, shape, dim)
+
+
+def quotient(x, n):
+    return x >> (n.bit_length() - 1) if n & (n - 1) == 0 else lax.div(x, jnp.int32(n))
+
+
+def remainder(x, n):
+    return x & (n - 1) if n & (n - 1) == 0 else lax.rem(x, jnp.int32(n))
+
+
+def flags(x):
+    return jnp.where(x, 1.0, 0.0).astype(bf16)
 
 
 def mm(a, b):
@@ -124,13 +136,11 @@
     def c_peer(k):
         return (2 * lax.rem(chip_at + 1 + k, chips) + core_at, narrow_at)
 
-    def w_peer(k):
-        return (lax.rem(wide_at + 1 + k, wide_count), narrow_at)
-
     east = (lax.rem(wide_at + 1, wide_count), narrow_at)
     west = (lax.rem(wide_at + wide_count - 1, wide_count), narrow_at)
     north = (wide_at, lax.rem(narrow_at + 1, narrow_count))
     south = (wide_at, lax.rem(narrow_at + narrow_count - 1, narrow_count))
+    twin = (2 * chip_at + 1 - core_at, narrow_at)
 
     loads = [
         pltpu.make_async_copy(a, b, in_sem.at[i])
@@ -161,7 +171,9 @@
         lax.fori_loop(0, number, one, 0)
 
     greet(z_peer, team - 1)
-    greet(w_peer, wide_count - 1)
+    greet(c_peer, chips - 1)
+    for device in (east, west):
+        pl.semaphore_signal(barrier, 1, device_id=device, device_id_type=MESH)
 
     for s in range(4):
         for t in range(4):
@@ -230,8 +242,8 @@
     )
 
     wide_lanes = 4 * lanes
-    grow = ((iota((2 * corner_rows, wide_lanes), 0) & (corner_rows - 1)) == iota((2 * corner_rows, wide_lanes), 1) // count).astype(f32).astype(bf16)
-    own_lane = iota((count, wide_lanes), 1) % count == iota((count, wide_lanes), 0)
+    grow = flags(remainder(iota((2 * corner_rows, wide_lanes), 0), corner_rows) == quotient(iota((2 * corner_rows, wide_lanes), 1), count))
+    own_lane = remainder(iota((count, wide_lanes), 1), count) == iota((count, wide_lanes), 0)
     own_lane_one = own_lane[:, 0:lanes]
 
     def restrict(pairs):
@@ -271,26 +283,26 @@
     loads[4].wait()
     from_lane = iota((order, lanes), 0)
     to_lane = iota((order, lanes), 1)
-    top = ((from_lane == to_lane) & (to_lane < order)).astype(f32).astype(bf16)
-    corner = ((from_lane == to_lane - half) & (to_lane >= order)).astype(f32).astype(bf16)
+    top = flags((from_lane == to_lane) & (to_lane < order))
+    corner = flags((from_lane == to_lane - half) & (to_lane >= order))
     packed[...] = fold(mm(halves(inverse[0:half, :]), top)) + fold(
         mm(halves(inverse[half:order, :]), corner)
     )
 
-    pl.semaphore_wait(barrier, team - 1 + wide_count - 1)
+    msg_at = iota((msg_rows, 8 * team), 0)
+    from_at = iota((msg_rows, 8 * team), 1)
+    from_row = from_at & 7
+    from_col = (from_at >> 3) & 1
+    from_sub = from_at >> 4
+    goes = (from_col + (from_row >> 1)) * verts + from_sub + (from_row & 1)
+    goes = jnp.where(from_row < 4, goes, jnp.where(from_row == 4, 3 * verts, -1))
+    merge = flags(msg_at == goes)
+
+    pl.semaphore_wait(barrier, team - 1 + chips - 1 + 2)
 
     def z_start(g):
         spread(f"z{g}", zmsg.at[g], zbuf.at[g], rank, z_send.at[g], z_recv.at[g], z_peer, team - 1)
         zbuf[g, rank] = zmsg[g]
-
-    msg_at = iota((msg_rows, 8 * team), 0)
-    from_at = iota((msg_rows, 8 * team), 1)
-    from_row = from_at & 7
-    from_col = (from_at // 8) & 1
-    from_sub = from_at // 16
-    goes = (from_col + from_row // 2) * verts + from_sub + (from_row & 1)
-    goes = jnp.where(from_row < 4, goes, jnp.where(from_row == 4, 3 * verts, -1))
-    merge = (msg_at == goes).astype(f32).astype(bf16)
 
     def w_start(g):
         arrive(f"z{g}")
@@ -302,40 +314,44 @@
     z_start(0)
     for f in range(2):
         single(f"fore{f}", fore_out.at[f], fore_in.at[f], fore_send.at[f], fore_recv.at[f], (east, north)[f])
-    spread("inv", packed, inverses, wide_at, inv_send, inv_recv, w_peer, wide_count - 1)
-    inverses[wide_at] = packed[...]
+    spread("inv", packed, inverses.at[core_at], chip_at, inv_send.at[0], inv_recv.at[0], c_peer, chips - 1)
+    inverses[core_at, chip_at] = packed[...]
 
     for copy in loads[5:]:
         copy.wait()
     for f in range(2):
-        perm[f] = (iota((width, width), 0) == match[f : f + 1, :]).astype(f32).astype(bf16)
+        perm[f] = flags(iota((width, width), 0) == match[f : f + 1, :])
     vertex = [
-        corners[wide_at, narrow_at],
-        corners[wide_at, narrow_at + 1],
-        corners[wide_at + 1, narrow_at],
-        corners[wide_at + 1, narrow_at + 1],
+        corners[narrow_at, wide_at],
+        corners[narrow_at + 1, wide_at],
+        corners[narrow_at, wide_at + 1],
+        corners[narrow_at + 1, wide_at + 1],
     ]
     owner = [lax.div(v, capacity) for v in vertex]
     place_in = [v - b * capacity for v, b in zip(vertex, owner)]
     total_rows = chips * msg_rows
-    row_at = iota((wide_count + 1, total_rows), 1)
-    in_msg = row_at % msg_rows
-    reach = (
-        (iota((wide_count + 1, total_rows), 0) == 2 * (row_at // msg_rows) + in_msg // verts) & (in_msg < 3 * verts)
-    ).astype(f32).astype(bf16)
-    same = (iota((16, verts), 0) == iota((16, verts), 1)).astype(f32).astype(bf16)
+    in_msg = remainder(iota((1, total_rows), 1), msg_rows)
+    in_col = (in_msg >= verts).astype(jnp.int32) + (in_msg >= 2 * verts).astype(jnp.int32)
+    column = 2 * quotient(iota((1, total_rows), 1), msg_rows) + in_col
+    column = jnp.where(in_msg < 3 * verts, column, -1)
+    reach = flags(iota((wide_count + 1, total_rows), 0) == column)
     each = 0.0
     for part in split(table[...].astype(f32)):
-        each = each + mm(mm_nt(same, part).astype(bf16), reach)
-    row_at = iota((16, total_rows), 1) % msg_rows
-    row_slots = jnp.sum(jnp.where(iota((16, total_rows), 0) == row_at % verts, each, 0.0), axis=0, keepdims=True)
-    row_slots = jnp.where(iota((1, total_rows), 1) % msg_rows < 3 * verts, row_slots, -1.0)
+        each = each + mm(part, reach)
+    row_slots = jnp.sum(jnp.where(iota((verts, total_rows), 0) == in_msg - verts * in_col, each, 0.0), axis=0, keepdims=True)
+    row_slots = jnp.where(in_msg < 3 * verts, row_slots, -1.0)
     for v in range(4):
-        wanted = (owner[v] * capacity + iota((order, 1), 0) // modes).astype(f32)
-        pick[v * order : (v + 1) * order, :] = (wanted == row_slots).astype(f32).astype(bf16)
-    pick[4 * order : 4 * order + 16, :] = (iota((16, total_rows), 1) % msg_rows == 3 * verts).astype(f32).astype(bf16)
+        wanted = (owner[v] * capacity + quotient(iota((order, 1), 0), modes)).astype(f32)
+        pick[v * order : (v + 1) * order, :] = flags(wanted == row_slots)
+    pick[4 * order : 4 * order + 16, :] = flags(jnp.broadcast_to(in_msg, (16, total_rows)) == 3 * verts)
 
     w_start(0)
+
+    def relay():
+        arrive("inv")
+        half_held = inverses.at[core_at]
+        single("relay", half_held, half_held, inv_send.at[1], inv_recv.at[1], twin)
+
 
     for f in range(2):
         arrive(f"fore{f}")
@@ -354,6 +370,7 @@
             jnp.concatenate(parts, axis=0).astype(bf16),
         )
     pltpu.make_async_copy(blocks, blocks, load_sem).wait()
+    relay()
 
     slot = [slots[0, d] for d in range(4)]
     base_out = []
@@ -382,20 +399,24 @@
             faces[d, 0:count].astype(f32) + faces[d, count : 2 * count].astype(f32)
         )
 
-    arrive("inv")
+    arrive("relay")
+    lane_at = iota((lanes, 2 * lanes), 1)
+    lane_mode = quotient(remainder(lane_at, lanes), count)
+    base_lane = iota((lanes, 2 * lanes), 0) - lane_mode - jnp.where(lane_at < lanes, 0, half)
+    row_at = iota((order, lanes), 0)
+    base_row = jnp.where(row_at < half, row_at, row_at - half) - quotient(iota((order, lanes), 1), count)
     for v in range(4):
-        column = place_in[v] * modes + iota((lanes, 2 * lanes), 1) % lanes // count
-        column = jnp.where(iota((lanes, 2 * lanes), 1) < lanes, column, column + half)
-        take = ((iota((lanes, 2 * lanes), 0) == column) & (place_in[v] * modes >= half)).astype(f32).astype(bf16)
-        across = ((iota((order, lanes), 0) % half == place_in[v] * modes + iota((order, lanes), 1) // count) & (place_in[v] * modes < half)).astype(f32).astype(bf16)
-        mine = halves(inverses[owner[v]])
+        first_at = place_in[v] * modes
+        take = flags(base_lane == jnp.where(first_at >= half, first_at, -order * lanes))
+        across = flags(base_row == jnp.where(first_at < half, first_at, -order * lanes))
+        mine = halves(inverses[lax.rem(owner[v], 2), lax.div(owner[v], 2)])
         right = fold(mm(mine, take))
         left = lax.dot_general(mine, across, (((0,), (0,)), ((), ())), preferred_element_type=f32)
         coef[v * order : v * order + half, :] = left[0:half] + right[:, 0:lanes]
         coef[v * order + half : (v + 1) * order, :] = left[half:order] + right[:, lanes:]
 
-    tile = ((iota((2 * lanes, lanes), 0) % count) == (iota((2 * lanes, lanes), 1) % count)).astype(f32).astype(bf16)
-    mode_lane = iota((4 * order, lanes), 1) // count == (iota((4 * order, lanes), 0) & (modes - 1))
+    tile = flags(remainder(iota((2 * lanes, lanes), 0), count) == remainder(iota((2 * lanes, lanes), 1), count))
+    mode_lane = quotient(iota((4 * order, lanes), 1), count) == remainder(iota((4 * order, lanes), 0), modes)
 
     def gathered(g):
         arrive(f"w{g}")
@@ -409,11 +430,12 @@
         ]
         return jnp.concatenate(rows, axis=1), picked[4 * order : 4 * order + 1]
 
-    shrink = (
-        (iota((wide_lanes, 4 * corner_rows), 0) // count == (iota((wide_lanes, 4 * corner_rows), 1) & (corner_rows - 1)))
-        & (iota((wide_lanes, 4 * corner_rows), 1) < 3 * corner_rows)
-    ).astype(f32).astype(bf16)
-    middle = iota((count, 4 * corner_rows), 1) // corner_rows == 1
+    to_small = iota((wide_lanes, 4 * corner_rows), 1)
+    shrink = flags(
+        (quotient(iota((wide_lanes, 4 * corner_rows), 0), count) == remainder(to_small, corner_rows))
+        & (to_small < 3 * corner_rows)
+    )
+    middle = quotient(iota((count, 4 * corner_rows), 1), corner_rows) == 1
 
     def lifted(correction):
         spread_out = jnp.where(own_lane, correction, 0.0)
@@ -539,10 +561,10 @@
             pltpu.VMEM((2, 2, modes, width), f32),
             pltpu.VMEM((order, order), f32),
             pltpu.VMEM((2, width), jnp.int32),
-            pltpu.VMEM((wide_count + 1, verts), jnp.int32),
+            pltpu.VMEM((verts, wide_count + 1), jnp.int32),
             pltpu.SMEM((1, 2), jnp.int32),
             pltpu.SMEM((1, 4), jnp.int32),
-            pltpu.SMEM((wide_count + 1, verts), jnp.int32),
+            pltpu.SMEM((verts, wide_count + 1), jnp.int32),
             pltpu.VMEM((4, 4, width, width), bf16),
             pltpu.VMEM((4, 2 * count + 2 * corner_rows, width), bf16),
             pltpu.VMEM((8, 4 * corner_rows, width), bf16),
@@ -550,7 +572,7 @@
             pltpu.VMEM((4 * order + 16, chips * msg_rows), bf16),
             pltpu.VMEM((4 * order, lanes), f32),
             pltpu.VMEM((order // 2, lanes), f32),
-            pltpu.VMEM((wide_count, order // 2, lanes), f32),
+            pltpu.VMEM((2, chips, order // 2, lanes), f32),
             pltpu.VMEM((2, 8, lanes), f32),
             pltpu.VMEM((2, team, 8, lanes), f32),
             pltpu.VMEM((2, msg_rows, lanes), f32),
@@ -577,22 +599,27 @@
             dma((2,)),
             dma((2, 2)),
             dma((2, 2)),
-            dma,
-            dma,
+            dma((2,)),
+            dma((2,)),
         ],
         compiler_params=pltpu.CompilerParams(
             collective_id=0, has_side_effects=True, vmem_limit_bytes=48 << 20
         ),
     )(
-        sources[0, 0],
-        schur[0, 0],
-        scaling[0, 0],
-        basis[0, 0],
-        inverse[0],
-        sizes[0],
-        match[0, 0],
-        slots[0],
-        corners,
+        *(
+            pltpu.with_memory_space_constraint(x, pltpu.HBM)
+            for x in (
+                sources[0, 0],
+                schur[0, 0],
+                scaling[0, 0],
+                basis[0, 0],
+                inverse[0],
+                sizes[0],
+                match[0, 0],
+                slots[0],
+                corners.T,
+            )
+        )
     )
     return sol[None, None], res[None, None]
 

time: 57.8 us -> 47.8 us (0.83)
  local copies, waits for them, and re-layouts: 7.19 us -> 1.26 us
  Pallas kernels: 49.6 us -> 45.7 us
    unnamed x17 -> x2, local copies, waits for them, and re-layouts: 7.19 us -> 1.26 us
    pallas_call x1, Pallas kernels: 49.6 us -> 45.7 us  [body(): pl.pallas_call(kernel, out_shape=(out, out), in_specs=[hbm] * 9, out_spec...]
where the time goes in v3:
time: 47.8 us; the launch traced here: 47.6 us
  Pallas kernels  45.7 us (96%)
  local copies, waits for them, and re-layouts  1.26 us (3%)
  between operations  0.64 us (1%)
    pallas_call x1, Pallas kernels, body(): pl.pallas_call(kernel, out_shape=(out, out), in_specs=[hbm] * 9, out_spec...  45.7 us
    unnamed x2, local copies, waits for them, and re-layouts  1.26 us

profile of v3, /device:TPU:1, one launch (start us, length us, event | category | flops | bytes accessed | tf_op | source)
XLA Modules:
  0.0 47.6 jit_solution(830874078658835807)
XLA Ops:
  0.6 45.7 %shard_map.104 = (f32[16,2,512]{2,1,0:T(2,128)S(1)}, f32[16,2,512]{2,1,0:T(2,128)S(1)}) custom-call(f32[16,2,512]{2,1,0:T(2,128)} %bitcast.14, bf16[2048,2048]{1,0:T(8,128)(2,1)} %bitcast.13, f32[2,512]{1,0:T(2,128)} %bitcast.18, f32[2,2,8,512]{3,2,1,0:T(8,128)} %bitcast.15, f32[80,80]{1,0:T(8,128)} %bitcast.16, s32[1,2]{1,0:T(1,128)} %bitcast.20, ...), custom_call_target="tpu_custom_call" | custom-call | tf_op jit(solution)/shard_map/pallas_call | solution.py:553
  46.4 0.6 %copy.13 = f32[1,1,16,2,512]{4,3,2,1,0:T(2,128)} copy(f32[1,1,16,2,512]{4,3,2,1,0:T(2,128)S(1)} %bitcast.12) | data formatting | bytes 131072
  47.0 0.6 %copy.14 = f32[1,1,16,2,512]{4,3,2,1,0:T(2,128)} copy(f32[1,1,16,2,512]{4,3,2,1,0:T(2,128)S(1)} %bitcast.11) | data formatting | bytes 131072

commit v4 on v3

--- a/solution.py
+++ b/solution.py
@@ -129,18 +129,40 @@
     team = 2 * narrow_count
     rank = 2 * narrow_at + core_at
 
+    side = 4
+    ring = chips // side
+
+    def around(t, size):
+        return size // 2 + lax.div(t, 2) * (1 - lax.rem(t, 2)) - lax.div(t + 1, 2) * lax.rem(t, 2)
+
     def z_peer(k):
-        other = lax.rem(rank + 1 + k, team)
-        return (2 * chip_at + lax.rem(other, 2), other // 2)
+        core = lax.rem(core_at + 1 + lax.rem(k, 2), 2)
+        return (2 * chip_at + core, lax.rem(narrow_at + around(lax.div(k, 2), narrow_count), narrow_count))
 
     def c_peer(k):
-        return (2 * lax.rem(chip_at + 1 + k, chips) + core_at, narrow_at)
+        x = lax.rem(lax.div(chip_at, side) + around(lax.div(k, side), ring), ring)
+        y = lax.rem(chip_at + around(lax.rem(k, side), side), side)
+        return (2 * (x * side + y) + core_at, narrow_at)
 
     east = (lax.rem(wide_at + 1, wide_count), narrow_at)
     west = (lax.rem(wide_at + wide_count - 1, wide_count), narrow_at)
     north = (wide_at, lax.rem(narrow_at + 1, narrow_count))
     south = (wide_at, lax.rem(narrow_at + narrow_count - 1, narrow_count))
     twin = (2 * chip_at + 1 - core_at, narrow_at)
+
+    barrier = pltpu.get_barrier_semaphore()
+
+    def greet(peer, number):
+        def one(k, carry):
+            pl.semaphore_signal(barrier, 1, device_id=peer(k), device_id_type=MESH)
+            return carry
+
+        lax.fori_loop(0, number, one, 0)
+
+    greet(z_peer, team - 1)
+    greet(c_peer, chips - 1)
+    for device in (east, west):
+        pl.semaphore_signal(barrier, 1, device_id=device, device_id_type=MESH)
 
     loads = [
         pltpu.make_async_copy(a, b, in_sem.at[i])
@@ -161,20 +183,6 @@
     for copy in loads:
         copy.start()
 
-    barrier = pltpu.get_barrier_semaphore()
-
-    def greet(peer, number):
-        def one(k, carry):
-            pl.semaphore_signal(barrier, 1, device_id=peer(k), device_id_type=MESH)
-            return carry
-
-        lax.fori_loop(0, number, one, 0)
-
-    greet(z_peer, team - 1)
-    greet(c_peer, chips - 1)
-    for device in (east, west):
-        pl.semaphore_signal(barrier, 1, device_id=device, device_id_type=MESH)
-
     for s in range(4):
         for t in range(4):
             pltpu.make_async_copy(
@@ -246,15 +254,21 @@
     own_lane = remainder(iota((count, wide_lanes), 1), count) == iota((count, wide_lanes), 0)
     own_lane_one = own_lane[:, 0:lanes]
 
-    def restrict(pairs):
+    def project(pairs):
         total = 0.0
         for values, d in pairs:
             total = total + mm_nt(
                 halves(values), faces[d, 2 * count : 2 * count + 2 * corner_rows, :]
             )
-        spread_out = fold(mm(halves(fold(total)), grow))
+        return fold(total)
+
+    def corner_rows_of(projected):
+        spread_out = fold(mm(halves(projected), grow))
         row = jnp.sum(jnp.where(own_lane, spread_out, 0.0), axis=0, keepdims=True)
         return jnp.concatenate([row[:, v * lanes : (v + 1) * lanes] for v in range(4)], axis=0)
+
+    def across_lanes(a, b):
+        return jnp.sum(a[:, 0 : 2 * corner_rows] * b, axis=1, keepdims=True)
 
     def inner(pairs):
         total = 0.0
@@ -277,7 +291,8 @@
     def as_row(value):
         return jnp.sum(jnp.where(own_lane_one, value, 0.0), axis=0, keepdims=True)
 
-    first = restrict([(residual[0], EAST), (residual[1], NORTH)])
+    start_coarse = project([(residual[0], EAST), (residual[1], NORTH)])
+    first = corner_rows_of(start_coarse)
     zmsg[0] = jnp.concatenate([first, jnp.zeros((4, lanes), f32)], axis=0)
 
     loads[4].wait()
@@ -375,6 +390,7 @@
     slot = [slots[0, d] for d in range(4)]
     base_out = []
     base_in = []
+    couple = 0.0
     for d in range(4):
         out = 0.0
         for s in range(4):
@@ -384,20 +400,30 @@
             out[2 * count : 2 * count + corner_rows]
             + out[2 * count + corner_rows : 2 * count + 2 * corner_rows]
         )
+        couple = couple + mm_nt(
+            jnp.concatenate([high, low], axis=0),
+            faces[d, 2 * count : 2 * count + 2 * corner_rows, :],
+        )
         lift[d, 0:corner_rows] = high
         lift[d, corner_rows : 2 * corner_rows] = high
         lift[d, 2 * corner_rows : 3 * corner_rows] = low
         lift[d, 3 * corner_rows :] = jnp.zeros((corner_rows, width), bf16)
-        high = faces[d, 2 * count : 2 * count + corner_rows]
-        lift[4 + d, 0:corner_rows] = high
-        lift[4 + d, corner_rows : 2 * corner_rows] = high
-        lift[4 + d, 2 * corner_rows : 3 * corner_rows] = faces[
-            d, 2 * count + corner_rows : 2 * count + 2 * corner_rows
-        ]
-        lift[4 + d, 3 * corner_rows :] = jnp.zeros((corner_rows, width), bf16)
+        if d < 2:
+            high = faces[d, 2 * count : 2 * count + corner_rows]
+            lift[4 + d, 0:corner_rows] = high
+            lift[4 + d, corner_rows : 2 * corner_rows] = high
+            lift[4 + d, 2 * corner_rows : 3 * corner_rows] = faces[
+                d, 2 * count + corner_rows : 2 * count + 2 * corner_rows
+            ]
+            lift[4 + d, 3 * corner_rows :] = jnp.zeros((corner_rows, width), bf16)
         base_in.append(
             faces[d, 0:count].astype(f32) + faces[d, count : 2 * count].astype(f32)
         )
+    high, low = split(fold(couple))
+    couple = jnp.concatenate([high, high, low, jnp.zeros_like(low)], axis=0)
+    base_coarse = project([(base_out[d], d) for d in range(4)])
+    base_inner = inner([(base_in[d], base_out[d]) for d in range(4)])
+    start_inner = inner([(residual[f], scaled[f]) for f in range(2)])
 
     arrive("relay")
     lane_at = iota((lanes, 2 * lanes), 1)
@@ -437,17 +463,24 @@
     )
     middle = quotient(iota((count, 4 * corner_rows), 1), corner_rows) == 1
 
-    def lifted(correction):
-        spread_out = jnp.where(own_lane, correction, 0.0)
-        small = fold(mm(halves(spread_out), shrink))
+    def shrunk(correction):
+        small = fold(mm(halves(jnp.where(own_lane, correction, 0.0)), shrink))
         high, low = split(small)
-        left = jnp.where(middle, low.astype(f32), high.astype(f32)).astype(bf16)
-        return [mm(left, lift[d]) for d in range(8)]
+        return small, jnp.where(middle, low.astype(f32), high.astype(f32)).astype(bf16)
 
     solved, _ = gathered(0)
-    added = lifted(solved)
-    direct = [base_in[d] + added[4 + d] for d in range(4)]
-    product = [base_out[d] + added[d] for d in range(4)]
+    small, left = shrunk(solved)
+    first_coarse = base_coarse + mm(left, couple)
+    sums = pack(
+        [
+            start_inner + across_lanes(small, start_coarse),
+            base_inner + across_lanes(small, base_coarse + first_coarse),
+        ]
+    )
+    zmsg[1] = jnp.concatenate(
+        [corner_rows_of(first_coarse), sums, jnp.zeros((3, lanes), f32)], axis=0
+    )
+    z_start(1)
 
     def to_owner(k, values):
         for f in range(2):
@@ -462,23 +495,19 @@
                 (west, south)[f],
             )
 
-    coarse = restrict([(product[d], d) for d in range(4)])
-    sums = pack(
-        [
-            inner([(residual[f], direct[f]) for f in range(2)]),
-            inner([(direct[d], product[d]) for d in range(4)]),
-        ]
-    )
-    zmsg[1] = jnp.concatenate([coarse, sums, jnp.zeros((3, lanes), f32)], axis=0)
-    z_start(1)
+    product = [base_out[d] + mm(left, lift[d]) for d in range(4)]
     to_owner(0, product[2:])
+    direct = [scaled[f] + mm(left, lift[4 + f]) for f in range(2)]
+    w_start(1)
     applied = []
     for f in range(2):
         arrive(f"back0{f}")
         applied.append((product[f] + back_in[0, f]) * live[f])
         flux_out[f] = halves(applied[f] * weight[f])
         single(f"flux{f}", flux_out.at[f], flux_in.at[f], flux_send.at[f], flux_recv.at[f], (east, north)[f])
-    w_start(1)
+    applied_coarse = project([(applied[f], f) for f in range(2)])
+    applied_inner = inner([(scaled[f], applied[f]) for f in range(2)])
+    applied_twice = inner([(applied[f] * weight[f], applied[f]) for f in range(2)])
     own_flux = [flux_out[f] for f in range(2)]
     for f in range(2):
         arrive(f"flux{f}")
@@ -490,28 +519,35 @@
             out = out + mm(own_flux[s], blocks[slot[s], slot[d]])
         flux_product.append(fold(out))
 
+    flux_coarse = project([(flux_product[d], d) for d in range(4)])
+    cross_inner = inner([(base_in[d], flux_product[d]) for d in range(4)])
+    flux_inner = inner([(fold(own_flux[d].astype(f32)), flux_product[d]) for d in range(4)])
+
     change, sums = gathered(1)
     product_start = unpack(sums, 0)
     curvature = unpack(sums, 1)
     step = product_start / curvature
     step_row = as_row(step)
     solved = solved - jnp.concatenate([step_row] * 4, axis=1) * change
-    added = lifted(solved)
-    fresh = [
-        base_in[d] - step * fold(own_flux[d].astype(f32)) + added[4 + d] for d in range(4)
-    ]
-    fresh_product = [base_out[d] - step * flux_product[d] + added[d] for d in range(4)]
+    small, left = shrunk(solved)
+    moved = mm(left, couple)
     residual = [residual[f] - step * applied[f] for f in range(2)]
+    weighted = [residual[f] * weight[f] for f in range(2)]
     zlast[...] = pack(
         [
-            inner([(residual[f], fresh[f]) for f in range(2)]),
-            inner([(fresh[d], fresh_product[d]) for d in range(4)]),
-            inner([(fresh[f], applied[f]) for f in range(2)]),
+            inner([(residual[f], weighted[f]) for f in range(2)])
+            + across_lanes(small, start_coarse - step * applied_coarse),
+            base_inner
+            - step * (2.0 * cross_inner - step * flux_inner)
+            + across_lanes(small, 2.0 * (base_coarse - step * flux_coarse) + moved),
+            applied_inner - step * applied_twice + across_lanes(small, applied_coarse),
         ]
     )
     spread("zlast", zlast, zlast_buf, rank, z_send.at[2], z_recv.at[2], z_peer, team - 1)
     zlast_buf[rank] = zlast[...]
+    fresh_product = [base_out[d] - step * flux_product[d] + mm(left, lift[d]) for d in range(4)]
     to_owner(1, fresh_product[2:])
+    fresh = [weighted[f] + mm(left, lift[4 + f]) for f in range(2)]
     arrive("zlast")
     wlast[...] = jnp.sum(zlast_buf[...], axis=0)
     spread("wlast", wlast, wlast_buf, chip_at, w_send.at[2], w_recv.at[2], c_peer, chips - 1)
@@ -567,7 +603,7 @@
             pltpu.SMEM((verts, wide_count + 1), jnp.int32),
             pltpu.VMEM((4, 4, width, width), bf16),
             pltpu.VMEM((4, 2 * count + 2 * corner_rows, width), bf16),
-            pltpu.VMEM((8, 4 * corner_rows, width), bf16),
+            pltpu.VMEM((6, 4 * corner_rows, width), bf16),
             pltpu.VMEM((2, width, width), bf16),
             pltpu.VMEM((4 * order + 16, chips * msg_rows), bf16),
             pltpu.VMEM((4 * order, lanes), f32),

time: 47.8 us -> 45.7 us (0.956)
  Pallas kernels: 45.7 us -> 43.7 us
    pallas_call x1, Pallas kernels: 45.7 us -> 43.7 us  [body(): pl.pallas_call(kernel, out_shape=(out, out), in_specs=[hbm] * 9, out_spec...]
where the time goes in v4:
time: 45.7 us; the launch traced here: 45.6 us
  Pallas kernels  43.7 us (96%)
  local copies, waits for them, and re-layouts  1.26 us (3%)
  between operations  0.64 us (1%)
    pallas_call x1, Pallas kernels, body(): pl.pallas_call(kernel, out_shape=(out, out), in_specs=[hbm] * 9, out_spec...  43.7 us
    unnamed x2, local copies, waits for them, and re-layouts  1.26 us

profile of v4, /device:TPU:1, one launch (start us, length us, event | category | flops | bytes accessed | tf_op | source)
XLA Modules:
  0.0 45.6 jit_solution(6629642339689993218)
XLA Ops:
  0.6 43.7 %shard_map.104 = (f32[16,2,512]{2,1,0:T(2,128)S(1)}, f32[16,2,512]{2,1,0:T(2,128)S(1)}) custom-call(f32[16,2,512]{2,1,0:T(2,128)} %bitcast.14, bf16[2048,2048]{1,0:T(8,128)(2,1)} %bitcast.13, f32[2,512]{1,0:T(2,128)} %bitcast.18, f32[2,2,8,512]{3,2,1,0:T(8,128)} %bitcast.15, f32[80,80]{1,0:T(8,128)} %bitcast.16, s32[1,2]{1,0:T(1,128)} %bitcast.20, ...), custom_call_target="tpu_custom_call" | custom-call | tf_op jit(solution)/shard_map/pallas_call | solution.py:589
  44.3 0.6 %copy.13 = f32[1,1,16,2,512]{4,3,2,1,0:T(2,128)} copy(f32[1,1,16,2,512]{4,3,2,1,0:T(2,128)S(1)} %bitcast.12) | data formatting | bytes 131072
  45.0 0.6 %copy.14 = f32[1,1,16,2,512]{4,3,2,1,0:T(2,128)} copy(f32[1,1,16,2,512]{4,3,2,1,0:T(2,128)S(1)} %bitcast.11) | data formatting | bytes 131072

commit v5 on v4

--- a/solution.py
+++ b/solution.py
@@ -60,8 +60,7 @@
     match_hbm,
     slots_hbm,
     corners_hbm,
-    sol_out,
-    res_out,
+    out_ref,
     src,
     scaling,
     basis,
@@ -132,17 +131,24 @@
     side = 4
     ring = chips // side
 
-    def around(t, size):
-        return size // 2 + lax.div(t, 2) * (1 - lax.rem(t, 2)) - lax.div(t + 1, 2) * lax.rem(t, 2)
-
-    def z_peer(k):
-        core = lax.rem(core_at + 1 + lax.rem(k, 2), 2)
-        return (2 * chip_at + core, lax.rem(narrow_at + around(lax.div(k, 2), narrow_count), narrow_count))
-
-    def c_peer(k):
-        x = lax.rem(lax.div(chip_at, side) + around(lax.div(k, side), ring), ring)
-        y = lax.rem(chip_at + around(lax.rem(k, side), side), side)
-        return (2 * (x * side + y) + core_at, narrow_at)
+    def around(size):
+        return sorted(range(size), key=lambda t: -min(t, size - t))
+
+    z_peers = [
+        (2 * chip_at + (lax.rem(core_at + c, 2) if c else core_at), lax.rem(narrow_at + t, narrow_count))
+        for t in around(narrow_count)
+        for c in (1, 0)
+        if t or c
+    ]
+    plane = [(a, b) for a in range(ring) for b in range(side) if a or b]
+    plane.sort(key=lambda at: -min(at[0], ring - at[0]) - min(at[1], side - at[1]))
+    c_peers = [
+        (
+            2 * (lax.rem(lax.div(chip_at, side) + a, ring) * side + lax.rem(chip_at + b, side)) + core_at,
+            narrow_at,
+        )
+        for a, b in plane
+    ]
 
     east = (lax.rem(wide_at + 1, wide_count), narrow_at)
     west = (lax.rem(wide_at + wide_count - 1, wide_count), narrow_at)
@@ -152,16 +158,7 @@
 
     barrier = pltpu.get_barrier_semaphore()
 
-    def greet(peer, number):
-        def one(k, carry):
-            pl.semaphore_signal(barrier, 1, device_id=peer(k), device_id_type=MESH)
-            return carry
-
-        lax.fori_loop(0, number, one, 0)
-
-    greet(z_peer, team - 1)
-    greet(c_peer, chips - 1)
-    for device in (east, west):
+    for device in z_peers + c_peers + [east, west]:
         pl.semaphore_signal(barrier, 1, device_id=device, device_id_type=MESH)
 
     loads = [
@@ -202,14 +199,17 @@
         part = ref.at[pl.ds(0, number)]
         pltpu.make_async_copy(part, part, sem).wait()
 
-    def spread(name, a, buf, at, send, recv, peer, number):
-        def one(k, carry):
-            remote(a, buf.at[at], send, recv, peer(k)).start()
-            return carry
-
-        lax.fori_loop(0, number, one, 0)
-        pending["send " + name] = lambda: wait_bytes(buf, number, send)
-        pending[name] = lambda: wait_bytes(buf, number, recv)
+    def spread(name, a, buf, at, send, recv, peers, rows=None):
+        to = buf.at[at]
+        held = buf
+        if rows is not None:
+            a, to, held = a.at[pl.ds(0, rows)], to.at[pl.ds(0, rows)], buf.at[:, pl.ds(0, rows)]
+
+        number = len(peers)
+        for peer in peers:
+            remote(a, to, send, recv, peer).start()
+        pending["send " + name] = lambda: wait_bytes(held, number, send)
+        pending[name] = lambda: wait_bytes(held, number, recv)
 
     def single(name, a, b, send, recv, device):
         copy = remote(a, b, send, recv, device)
@@ -291,6 +291,11 @@
     def as_row(value):
         return jnp.sum(jnp.where(own_lane_one, value, 0.0), axis=0, keepdims=True)
 
+    for g in range(2):
+        zbuf[g, :, 4 + g : 8, :] = jnp.zeros((team, 4 - g, lanes), f32)
+        wbuf[g, :, 3 * verts + g : msg_rows, :] = jnp.zeros(
+            (chips, msg_rows - 3 * verts - g, lanes), f32
+        )
     start_coarse = project([(residual[0], EAST), (residual[1], NORTH)])
     first = corner_rows_of(start_coarse)
     zmsg[0] = jnp.concatenate([first, jnp.zeros((4, lanes), f32)], axis=0)
@@ -313,23 +318,23 @@
     goes = jnp.where(from_row < 4, goes, jnp.where(from_row == 4, 3 * verts, -1))
     merge = flags(msg_at == goes)
 
-    pl.semaphore_wait(barrier, team - 1 + chips - 1 + 2)
+    pl.semaphore_wait(barrier, len(z_peers) + len(c_peers) + 2)
 
     def z_start(g):
-        spread(f"z{g}", zmsg.at[g], zbuf.at[g], rank, z_send.at[g], z_recv.at[g], z_peer, team - 1)
+        spread(f"z{g}", zmsg.at[g], zbuf.at[g], rank, z_send.at[g], z_recv.at[g], z_peers, 4 + g)
         zbuf[g, rank] = zmsg[g]
 
     def w_start(g):
         arrive(f"z{g}")
         high, low = split(zbuf[g].reshape(8 * team, lanes))
         wmsg[g] = mm(merge, high) + mm(merge, low)
-        spread(f"w{g}", wmsg.at[g], wbuf.at[g], chip_at, w_send.at[g], w_recv.at[g], c_peer, chips - 1)
+        spread(f"w{g}", wmsg.at[g], wbuf.at[g], chip_at, w_send.at[g], w_recv.at[g], c_peers, 3 * verts + g)
         wbuf[g, chip_at] = wmsg[g]
 
     z_start(0)
     for f in range(2):
         single(f"fore{f}", fore_out.at[f], fore_in.at[f], fore_send.at[f], fore_recv.at[f], (east, north)[f])
-    spread("inv", packed, inverses.at[core_at], chip_at, inv_send.at[0], inv_recv.at[0], c_peer, chips - 1)
+    spread("inv", packed, inverses.at[core_at], chip_at, inv_send.at[0], inv_recv.at[0], c_peers)
     inverses[core_at, chip_at] = packed[...]
 
     for copy in loads[5:]:
@@ -543,14 +548,14 @@
             applied_inner - step * applied_twice + across_lanes(small, applied_coarse),
         ]
     )
-    spread("zlast", zlast, zlast_buf, rank, z_send.at[2], z_recv.at[2], z_peer, team - 1)
+    spread("zlast", zlast, zlast_buf, rank, z_send.at[2], z_recv.at[2], z_peers)
     zlast_buf[rank] = zlast[...]
     fresh_product = [base_out[d] - step * flux_product[d] + mm(left, lift[d]) for d in range(4)]
     to_owner(1, fresh_product[2:])
     fresh = [weighted[f] + mm(left, lift[4 + f]) for f in range(2)]
     arrive("zlast")
     wlast[...] = jnp.sum(zlast_buf[...], axis=0)
-    spread("wlast", wlast, wlast_buf, chip_at, w_send.at[2], w_recv.at[2], c_peer, chips - 1)
+    spread("wlast", wlast, wlast_buf, chip_at, w_send.at[2], w_recv.at[2], c_peers)
     wlast_buf[chip_at] = wlast[...]
     fresh_applied = []
     for f in range(2):
@@ -563,8 +568,8 @@
     last_curvature = unpack(sums, 1) + 2.0 * ratio * unpack(sums, 2) + ratio * ratio * curvature
     last_step = product_fresh / last_curvature
     for f in range(2):
-        sol_out[:, f, :] = step * direct[f] + last_step * (fresh[f] + ratio * direct[f])
-        res_out[:, f, :] = residual[f] - last_step * (fresh_applied[f] + ratio * applied[f])
+        out_ref[0, :, f, :] = step * direct[f] + last_step * (fresh[f] + ratio * direct[f])
+        out_ref[1, :, f, :] = residual[f] - last_step * (fresh_applied[f] + ratio * applied[f])
 
     for wait in list(pending.values()):
         wait()
@@ -584,13 +589,13 @@
     vmem = pl.BlockSpec(memory_space=pltpu.VMEM)
     hbm = pl.BlockSpec(memory_space=pltpu.HBM)
     dma = pltpu.SemaphoreType.DMA
-    out = jax.ShapeDtypeStruct((count, 2, width), f32)
+    out = jax.ShapeDtypeStruct((2, count, 2, width), f32)
     corner_rows = 4 * modes
-    sol, res = pl.pallas_call(
+    both = pl.pallas_call(
         kernel,
-        out_shape=(out, out),
+        out_shape=out,
         in_specs=[hbm] * 9,
-        out_specs=(vmem, vmem),
+        out_specs=vmem,
         scratch_shapes=[
             pltpu.VMEM((count, 2, width), f32),
             pltpu.VMEM((2, width), f32),
@@ -657,7 +662,7 @@
             )
         )
     )
-    return sol[None, None], res[None, None]
+    return both[0][None, None], both[1][None, None]
 
 
 def solution(mesh):

time: 45.7 us -> 43.7 us (0.956)
  Pallas kernels: 43.7 us -> 42.1 us
  local copies, waits for them, and re-layouts: 1.26 us -> 0.66 us
    pallas_call x1, Pallas kernels: 43.7 us -> 42.1 us  [body(): pl.pallas_call(kernel, out_shape=out, in_specs=[hbm] * 9, out_specs=vmem,...]
    unnamed x2 -> x0, local copies, waits for them, and re-layouts: 1.26 us -> none
    another operation x0 -> x1, local copies, waits for them, and re-layouts: none -> 0.66 us  [body(): return (both[0][None, None], both[1][None, None])]
where the time goes in v5:
time: 43.7 us; the launch traced here: 43.4 us
  Pallas kernels  42.1 us (96%)
  local copies, waits for them, and re-layouts  0.66 us (2%)
  between operations  0.64 us (1%)
    pallas_call x1, Pallas kernels, body(): pl.pallas_call(kernel, out_shape=out, in_specs=[hbm] * 9, out_specs=vmem,...  42.1 us

profile of v5, /device:TPU:1, one launch (start us, length us, event | category | flops | bytes accessed | tf_op | source)
XLA Modules:
  0.0 43.4 jit_solution(8630369981468374676)
XLA Ops:
  0.6 42.1 %shard_map.104 = f32[2,16,2,512]{3,2,1,0:T(2,128)S(1)} custom-call(f32[16,2,512]{2,1,0:T(2,128)} %bitcast.14, bf16[2048,2048]{1,0:T(8,128)(2,1)} %bitcast.13, f32[2,512]{1,0:T(2,128)} %bitcast.18, f32[2,2,8,512]{3,2,1,0:T(8,128)} %bitcast.15, f32[80,80]{1,0:T(8,128)} %bitcast.16, s32[1,2]{1,0:T(1,128)} %bitcast.20, s32[2,512]{1,0:T(2,128)} %bitcast.19, ...), custom_call_target="tpu_custom_call" | custom-call | tf_op jit(solution)/shard_map/pallas_call | solution.py:594
  42.7 0.7 %slice_bitcast_fusion = (f32[1,1,16,2,512]{4,3,2,1,0:T(2,128)}, f32[1,1,16,2,512]{4,3,2,1,0:T(2,128)}) fusion(f32[2,16,2,512]{3,2,1,0:T(2,128)S(1)} %shard_map.104), kind=kLoop, calls=%fused_computation | loop fusion | bytes 262144 | tf_op jit(solution)/shard_map/broadcast_in_dim;squeeze | solution.py:665
